TPU v7x, 32 devices: a whole 2x2x4 slice. The times are simulated.
32 devices in a mesh: vis: 8 (over y, x, core), wav: 4 (over z).
Axes of the slice: x: 2, y: 2, z: 4, core: 2. Of those that a mesh axis runs over, the one named last changes fastest.
Arguments:
- image: float32 [4096, 4096], P('vis', 'wav'), may hold values from -6 to 6
- kernel_v: bfloat16 [1024, 64, 256], P(('vis', 'wav')), may hold values from -0.5 to 0.5
- kernel_u: bfloat16 [1024, 64, 256], P(('vis', 'wav')), may hold values from -0.5 to 0.5
- measured: bfloat16 [1024, 2, 256], P(('vis', 'wav')), may hold values from -4 to 4
- dest_owner: int32 [1024, 1], P(('vis', 'wav')), may hold values from 0 to 7; in each aligned block of 32 rows (0 to 31, 32 to 63, ...) at most 8 rows name the same one
- patch_slot: int32 [1024], P(('vis', 'wav')), may hold values from 0 to 127
- thresholds: float32 [4], replicated, may hold values from 0.1 to 1
Outputs:
- restored: float32 [4096, 4096], P('vis', 'wav')
- residual: float32 [1024, 2, 256], P(('vis', 'wav'))
Inputs may be any that keep to these rules, and one draw needn't show every extreme that they name: `dest_owner`: the vis index of the owner of the block's uv cells; the 32 blocks of one device name one owner at most 8 times, a bound that some block reaches. `patch_slot`: the block's kernel block among the 128 of its owner's tile in the band of the block's wav index.
All inputs are finite; a program needn't handle non-finite values.
Results may differ from a plain program's by a relative error of at most 0.0017.
Values may be sent and summed in bfloat16 or wider, within the bound.
No kernel may reach another device: no remote copies, remote signals or barrier semaphores. Data moves between devices by JAX's collectives and lax.ppermute only.
A program may use at most 128 MiB of HBM per device.

v0:
```python
import math

import jax
import jax.numpy as jnp
import numpy as np
from jax import lax
from jax.sharding import PartitionSpec as P

IMG = 4096
PATCH = 64
FA = 64
FB = 64


HIGHEST = lax.Precision.HIGHEST


def haar_table():
    rows = np.zeros((8, 8))
    root = 1.0 / np.sqrt(8.0)
    rows[0, :] = root
    rows[1, :4] = root
    rows[1, 4:] = -root
    rows[2, 0:2] = 0.5
    rows[2, 2:4] = -0.5
    rows[3, 4:6] = 0.5
    rows[3, 6:8] = -0.5
    for index in range(4):
        rows[4 + index, 2 * index] = np.sqrt(0.5)
        rows[4 + index, 2 * index + 1] = -np.sqrt(0.5)
    return np.kron(np.eye(16), rows)


def basis_prox(field, shift, limit, table):
    height, width = field.shape
    moved = jnp.roll(field, -shift, axis=1).reshape(height, width // 128, 128)
    coeff = jnp.einsum("rgj,kj->rgk", moved, table, precision=HIGHEST)
    coeff = coeff.reshape(height // 2, 2, width // 128, 128)
    factor = math.sqrt(0.5)
    upper = (coeff[:, 0] + coeff[:, 1]) * factor
    lower = (coeff[:, 0] - coeff[:, 1]) * factor
    upper = upper - jnp.clip(upper, -limit, limit)
    lower = lower - jnp.clip(lower, -limit, limit)
    coeff = jnp.stack([(upper + lower) * factor, (upper - lower) * factor], 1)
    coeff = coeff.reshape(height, width // 128, 128)
    back = jnp.einsum("rgk,kj->rgj", coeff, table, precision=HIGHEST)
    return jnp.roll(back.reshape(height, width), shift, axis=1)


def dft_tables(sign):
    first_idx = jnp.arange(FA, dtype=jnp.int32)
    second_idx = jnp.arange(FB, dtype=jnp.int32)
    first_angle = (first_idx[:, None] * first_idx[None, :] % FA).astype(jnp.float32) * (
        2.0 * math.pi / FA
    )
    twist_angle = (first_idx[:, None] * second_idx[None, :] % IMG).astype(jnp.float32) * (
        2.0 * math.pi / IMG
    )
    second_angle = (second_idx[:, None] * second_idx[None, :] % FB).astype(jnp.float32) * (
        2.0 * math.pi / FB
    )
    return (
        jnp.cos(first_angle),
        sign * jnp.sin(first_angle),
        jnp.cos(twist_angle),
        sign * jnp.sin(twist_angle),
        jnp.cos(second_angle),
        sign * jnp.sin(second_angle),
    )


def dft_last(real_part, imag_part, tables, want_imag):
    first_cos, first_sin, twist_cos, twist_sin, second_cos, second_sin = tables
    leading = real_part.shape[:-1]
    real_in = real_part.reshape(leading + (FA, FB))
    mix_real = jnp.einsum("ka,...ab->...kb", first_cos, real_in, precision=HIGHEST)
    mix_imag = jnp.einsum("ka,...ab->...kb", first_sin, real_in, precision=HIGHEST)
    if imag_part is not None:
        imag_in = imag_part.reshape(leading + (FA, FB))
        mix_real = mix_real - jnp.einsum("ka,...ab->...kb", first_sin, imag_in, precision=HIGHEST)
        mix_imag = mix_imag + jnp.einsum("ka,...ab->...kb", first_cos, imag_in, precision=HIGHEST)
    turned_real = mix_real * twist_cos - mix_imag * twist_sin
    turned_imag = mix_real * twist_sin + mix_imag * twist_cos
    factor = 1.0 / math.sqrt(IMG)
    out_real = jnp.einsum("...kb,jb->...jk", turned_real, second_cos, precision=HIGHEST)
    out_real = out_real - jnp.einsum("...kb,jb->...jk", turned_imag, second_sin, precision=HIGHEST)
    out_real = out_real.reshape(leading + (IMG,)) * factor
    if not want_imag:
        return (out_real, None)
    out_imag = jnp.einsum("...kb,jb->...jk", turned_real, second_sin, precision=HIGHEST)
    out_imag = out_imag + jnp.einsum("...kb,jb->...jk", turned_imag, second_cos, precision=HIGHEST)
    return (out_real, out_imag.reshape(leading + (IMG,)) * factor)


def degrid_values(v_side_length, u_side_length, grid_patch, measurements):
    product = jnp.einsum(
        "nac,nat->nct", grid_patch, v_side_length, preferred_element_type=jnp.float32
    )
    width = u_side_length.shape[1]
    sky_model_real = jnp.sum(product[:, :width] * u_side_length, 1)
    sky_model_imag = jnp.sum(product[:, width:] * u_side_length, 1)
    return jnp.stack([sky_model_real, sky_model_imag], 1) - measurements.astype(jnp.float32)


def grid_terms(v_side_length, u_side_length, misfit):
    weighted = jnp.concatenate(
        [misfit[:, 0, None, :] * u_side_length, misfit[:, 1, None, :] * u_side_length], 1
    ).astype(jnp.bfloat16)
    return jnp.einsum("nat,nct->nac", v_side_length, weighted, preferred_element_type=jnp.float32)


def shards(image, kernel_v, kernel_u, measured, dest_owner, patch_slot, thresholds):
    vis_count = lax.axis_size("vis")
    wav_count = lax.axis_size("wav")
    block_count = kernel_v.shape[0]
    capacity = 2 * block_count // vis_count
    slot_total = capacity * vis_count
    strip = IMG // (vis_count * wav_count)
    kv_size = IMG // vis_count
    ku_size = IMG // wav_count
    tile_down = kv_size // PATCH
    tile_across = ku_size // PATCH
    patch_count = tile_down * tile_across
    table = jnp.asarray(haar_table(), jnp.float32)
    forward_tables = dft_tables(-1.0)
    inverse_tables = dft_tables(1.0)
    target_device = dest_owner[:, 0]
    member = (target_device[:, None] == jnp.arange(vis_count, dtype=jnp.int32)[None, :]).astype(
        jnp.int32
    )
    earlier = jnp.cumsum(member, axis=0) - member
    position = target_device * capacity + jnp.sum(earlier * member, axis=1)
    slot_ids = (
        jnp.zeros((slot_total, 1), jnp.bfloat16)
        .at[position]
        .set(patch_slot[:, None].astype(jnp.bfloat16))
    )
    pack_v = jnp.zeros((slot_total,) + kernel_v.shape[1:], jnp.bfloat16).at[position].set(kernel_v)
    pack_u = jnp.zeros((slot_total,) + kernel_u.shape[1:], jnp.bfloat16).at[position].set(kernel_u)
    packed_measurements = (
        jnp.zeros((slot_total,) + measured.shape[1:], jnp.bfloat16).at[position].set(measured)
    )
    received_v_coords, received_u_coords, received_measurements, received_ids = (
        lax.all_to_all(pack_v, "vis", split_axis=0, concat_axis=0, tiled=True),
        lax.all_to_all(pack_u, "vis", split_axis=0, concat_axis=0, tiled=True),
        lax.all_to_all(packed_measurements, "vis", split_axis=0, concat_axis=0, tiled=True),
        lax.all_to_all(slot_ids, "vis", split_axis=0, concat_axis=0, tiled=True),
    )
    owning_device_ids = received_ids[:, 0].astype(jnp.int32)
    misfit = None
    estimate = image
    wav_index = lax.axis_index("wav")
    real_part, imag_part = dft_last(
        lax.all_to_all(estimate, "wav", split_axis=0, concat_axis=1, tiled=True),
        None,
        forward_tables,
        True,
    )
    stacked = jnp.stack([real_part, imag_part], 0)
    moved = lax.all_to_all(
        lax.all_to_all(stacked, "vis", split_axis=2, concat_axis=1, tiled=True),
        "wav",
        split_axis=2,
        concat_axis=1,
        tiled=True,
    )
    moved = (
        moved.reshape(2, wav_count, vis_count, strip, strip)
        .transpose(0, 4, 2, 1, 3)
        .reshape(2, strip, IMG)
    )
    real_part, imag_part = dft_last(moved[0], moved[1], forward_tables, True)
    blocks = (
        lax.all_to_all(
            jnp.stack([real_part, imag_part], 0).astype(jnp.bfloat16),
            "wav",
            split_axis=2,
            concat_axis=1,
            tiled=True,
        )
        .astype(jnp.float32)
        .reshape(2, tile_down, PATCH, tile_across, PATCH)
        .transpose(1, 3, 2, 0, 4)
    )
    misfit = degrid_values(
        received_v_coords,
        received_u_coords,
        blocks.reshape(patch_count, PATCH, 2 * PATCH).astype(jnp.bfloat16)[owning_device_ids],
        received_measurements,
    )
    onehot = (
        owning_device_ids[:, None] == jnp.arange(patch_count, dtype=jnp.int32)[None, :]
    ).astype(jnp.float32)
    summed = jnp.einsum(
        "sq,sac->qac",
        onehot,
        grid_terms(received_v_coords, received_u_coords, misfit),
        precision=HIGHEST,
    )
    blocks = summed.reshape(tile_down, tile_across, PATCH, 2, PATCH).transpose(3, 0, 2, 1, 4)
    grid_grad = blocks.reshape(2, kv_size, ku_size)
    moved = lax.all_to_all(
        grid_grad.astype(jnp.bfloat16), "wav", split_axis=1, concat_axis=2, tiled=True
    ).astype(grid_grad.dtype)
    real_part, imag_part = dft_last(moved[0], moved[1], inverse_tables, True)
    stacked = jnp.stack([real_part, imag_part], 0).transpose(0, 2, 1)
    moved = lax.all_to_all(
        lax.all_to_all(
            stacked.astype(jnp.bfloat16), "vis", split_axis=1, concat_axis=2, tiled=True
        ),
        "wav",
        split_axis=1,
        concat_axis=2,
        tiled=True,
    ).astype(stacked.dtype)
    moved = (
        moved.reshape(2, strip, wav_count, vis_count, strip)
        .transpose(0, 1, 3, 2, 4)
        .reshape(2, strip, IMG)
    )
    gradient = lax.all_to_all(
        dft_last(moved[0], moved[1], inverse_tables, False)[0].astype(jnp.bfloat16),
        "wav",
        split_axis=1,
        concat_axis=0,
        tiled=True,
    ).astype(jnp.float32)
    gathered = lax.all_gather(estimate - gradient, "wav", axis=1, tiled=True)
    single = basis_prox(gathered, wav_index, thresholds[wav_index], table)
    estimate = lax.psum_scatter(single, "wav", scatter_dimension=1, tiled=True) * (1.0 / wav_count)
    returned = lax.all_to_all(misfit, "vis", split_axis=0, concat_axis=0, tiled=True)
    residual = returned[position]
    return (estimate, residual)


def solution(mesh):
    in_specs = (
        P("vis", "wav"),
        P(("vis", "wav"), None, None),
        P(("vis", "wav"), None, None),
        P(("vis", "wav"), None, None),
        P(("vis", "wav"), None),
        P(("vis", "wav")),
        P(),
    )
    out_specs = (P("vis", "wav"), P(("vis", "wav"), None, None))
    return jax.shard_map(shards, mesh=mesh, in_specs=in_specs, out_specs=out_specs, check_vma=False)
```

profile of v0, /device:TPU:2, one launch (start us, length us, event | category | flops | bytes accessed | tf_op | source)
XLA Modules:
  0.0 1093.5 jit_solution(5774231187537844015)
XLA Ops:
  7.2 4.9 all-to-all-start.2
  12.5 47.7 %all-to-all-done.2 = f32[4,128,1024]{2,1,0:T(8,128)S(1)} async-done(((f32[4,128,1024]{2,1,0:T(8,128)}), f32[4,128,1024]{2,1,0:T(8,128)S(1)}, u32[]{:S(2)}, u32[]{:S(2)}) %all-to-all-start.2) | async-done | bytes 2097184 | tf_op jit(solution)/shard_map/all_to_all | solution.py:154
  66.6 4.2 subtract_bitcast_fusion
  86.5 15.6 %copy.220 = f32[2,128,4096]{1,0,2:T(2,128)S(1)} copy(f32[2,128,4096]{1,2,0:T(8,128)S(1)} %pad_maximum_fusion.1) | data formatting | bytes 8388608 | tf_op jit(solution)/shard_map/stack | solution.py:159
  102.2 51.6 %all_to_all.146 = f32[2,128,4096]{1,0,2:T(2,128)S(1)} all-to-all(f32[2,128,4096]{1,0,2:T(2,128)S(1)} %copy.220), channel_id=1, replica_groups=mesh['vis'=8,'wav'=4] {'vis'}, dimensions={2} | all-to-all | bytes 8388608 | tf_op jit(solution)/shard_map/all_to_all | solution.py:161
  156.1 5.3 copy.222
  161.4 7.4 copy.223
  168.8 5.0 all-to-all-start.4
  174.2 10.1 scatter_custom_fusion
  186.9 80.4 %all-to-all-done.4 = f32[2,1024,512]{1,0,2:T(2,128)} async-done(((f32[2,1024,512]{1,0,2:T(2,128)}), f32[2,1024,512]{1,0,2:T(2,128)}, u32[]{:S(2)}, u32[]{:S(2)}) %all-to-all-start.4) | async-done | bytes 4194336 | tf_op jit(solution)/shard_map/all_to_all | solution.py:160
  267.3 4.1 all-to-all-start
  271.4 5.5 copy.224
  276.9 5.3 copy.225
  295.4 6.3 fusion.19
  301.7 4.3 all-to-all-start.1
  306.0 4.6 fusion.35
  318.6 3.7 fusion.86
  323.2 18.1 %copy.240 = bf16[2,128,4096]{1,0,2:T(2,128)(2,1)} copy(bf16[2,128,4096]{1,2,0:T(8,128)(2,1)S(1)} %pad_maximum_fusion.2) | data formatting | bytes 4194304 | tf_op jit(solution)/shard_map/stack | solution.py:175
  341.3 4.5 all-to-all-start.5
  349.9 44.6 %all-to-all-done.5 = bf16[2,128,4096]{1,0,2:T(2,128)(2,1)} async-done(((bf16[2,128,4096]{1,0,2:T(2,128)(2,1)}), bf16[2,128,4096]{1,0,2:T(2,128)(2,1)}, u32[]{:S(2)}, u32[]{:S(2)}) %all-to-all-start.5) | async-done | bytes 2097184 | tf_op jit(solution)/shard_map/all_to_all | solution.py:174
  394.6 4.4 all-to-all-start.6
  399.7 4.2 scatter_fusion.2
  404.1 6.2 copy.241
  410.2 6.4 convert_element_type.212
  416.6 8.5 copy.242
  425.1 7.8 convert_element_type.214
  435.3 6.1 fusion.334
  441.4 4.6 all-to-all-start.7
  446.1 5.2 fusion.7
  464.3 5.0 copy.391
  469.3 5.5 convert_element_type.222
  482.2 48.5 %all-to-all-done.8 = bf16[2,512,1024]{2,0,1:T(2,128)(2,1)S(1)} async-done(((bf16[2,512,1024]{2,0,1:T(2,128)(2,1)}), bf16[2,512,1024]{2,0,1:T(2,128)(2,1)S(1)}, u32[]{:S(2)}, u32[]{:S(2)}) %all-to-all-start.8) | async-done | bytes 2097184 | tf_op jit(solution)/shard_map/all_to_all | solution.py:202
  558.1 17.8 %copy.260 = bf16[2,4096,128]{2,0,1:T(2,128)(2,1)S(1)} copy(bf16[2,4096,128]{2,1,0:T(8,128)(2,1)S(1)} %maximum_bitcast_fusion) | data formatting | bytes 4194304 | tf_op jit(solution)/shard_map/convert_element_type | solution.py:209
  576.0 29.1 %all_to_all.147 = bf16[2,4096,128]{2,0,1:T(2,128)(2,1)S(1)} all-to-all(bf16[2,4096,128]{2,0,1:T(2,128)(2,1)S(1)} %copy.260), channel_id=1, replica_groups=mesh['vis'=8,'wav'=4] {'vis'}, dimensions={1} | all-to-all | bytes 4194304 | tf_op jit(solution)/shard_map/all_to_all | solution.py:208
  607.9 5.0 copy.263
  613.0 51.0 %all_to_all.148 = bf16[2,512,1024]{2,0,1:T(2,128)(2,1)S(1)} all-to-all(bf16[2,512,1024]{2,0,1:T(2,128)(2,1)S(1)} %copy.263), channel_id=1, replica_groups=mesh['vis'=8,'wav'=4] {'wav'}, dimensions={1} | all-to-all | bytes 4194304 | tf_op jit(solution)/shard_map/all_to_all | solution.py:207
  684.3 27.8 %all_to_all.149 = bf16[128,4,1024]{0,2,1:T(8,128)(2,1)S(1)} all-to-all(bf16[128,4,1024]{0,2,1:T(8,128)(2,1)S(1)} %bitcast.254), channel_id=1, replica_groups=mesh['vis'=8,'wav'=4] {'wav'}, dimensions={1} | all-to-all | bytes 2097152 | tf_op jit(solution)/shard_map/all_to_all | solution.py:221
  721.8 146.0 %all-gather.2.cloned.1.call-done = f32[512,4096]{1,0:T(8,128)} async-done(((f32[512,1024]{1,0:T(8,128)}), f32[512,4096]{1,0:T(8,128)}) %all-gather.2.cloned.1.call-update) | async-done | bytes 8388624 | tf_op jit(solution)/shard_map/all_gather | solution.py:228
  867.8 11.0 %fusion.2 = f32[64,8,32,128]{3,1,2,0:T(8,128)} fusion(s32[]{:T(128)S(6)} %select_n.151, f32[512,4096]{1,0:T(8,128)} %all-gather.2.cloned.1.call-done), kind=kLoop, calls=%fused_computation.12 | loop fusion | flops 2097152 | bytes 16777220
  878.8 5.2 copy.287
  884.1 13.3 %fusion.5 = f32[256,2,32,128]{3,0,2,1:T(8,128)S(1)} fusion(f32[128,128,1,1]{1,0,3,2:T(8,128)S(1)} %copy-done.9, f32[256,2,32,128]{3,2,1,0:T(8,128)S(1)} %bitcast.221), kind=kOutput, calls=%fused_computation.16 | convolution fusion | flops 3221225472 | bytes 16842752 | tf_op jit(solution)/shard_map/rgj,kj->rgk/dot_general | solution.py:37
  901.3 4.9 copy.277
  906.2 13.4 %fusion.3 = f32[512,32,128]{0,2,1:T(8,128)} fusion(f32[128,128,1]{1,0,2:T(8,128)S(1)} %copy-done.8, f32[512,32,128]{2,1,0:T(8,128)S(1)} %bitcast.222), kind=kOutput, calls=%fused_computation.14 | convolution fusion | flops 3221225472 | bytes 16842752 | tf_op jit(solution)/shard_map/rgk,kj->rgj/dot_general | solution.py:46
  919.6 9.2 copy.280
  928.8 11.0 %fusion = f32[512,4096]{1,0:T(8,128)} fusion(s32[]{:T(128)S(6)} %select_n.153, f32[512,4096]{1,0:T(8,128)} %copy.280), kind=kLoop, calls=%fused_computation.10 | loop fusion | flops 2097152 | bytes 16777220 | tf_op jit(solution)/shard_map/jit(_roll_dynamic)/concatenate | solution.py:47
  939.9 4.2 all-to-all-start.12
  944.1 4.0 all-to-all-done.12
  949.4 133.5 %reduce-scatter.2.cloned.1.call-done = f32[512,1024]{1,0:T(8,128)} async-done(((f32[512,4096]{1,0:T(8,128)}), f32[512,1024]{1,0:T(8,128)}) %reduce-scatter.2.cloned.1.call-update) | async-done | bytes 2097168 | tf_op jit(solution)/shard_map/reduce_scatter | solution.py:230
  (130 shorter events, 145.1 us)
Async XLA Ops:
  7.2 53.1 %all-to-all-start.2 = ((f32[4,128,1024]{2,1,0:T(8,128)}), f32[4,128,1024]{2,1,0:T(8,128)S(1)}, u32[]{:S(2)}, u32[]{:S(2)}) async-start(f32[4,128,1024]{2,1,0:T(8,128)} %bitcast.244), calls=%async_computation.2 | async-start | bytes 4194304 | tf_op jit(solution)/shard_map/all_to_all | solution.py:154
  60.2 1.3 copy-start.4
  168.8 5.0 copy-start.12
  168.8 5.0 copy-start.11
  168.8 98.5 %all-to-all-start.4 = ((f32[2,1024,512]{1,0,2:T(2,128)}), f32[2,1024,512]{1,0,2:T(2,128)}, u32[]{:S(2)}, u32[]{:S(2)}) async-start(f32[2,1024,512]{1,0,2:T(2,128)} %copy.223), calls=%async_computation.4 | async-start | bytes 8388608 | tf_op jit(solution)/shard_map/all_to_all | solution.py:160
  173.8 11.4 %copy-start.6 = (bf16[32,64,256]{2,1,0:T(8,128)(2,1)S(1)}, bf16[32,64,256]{2,1,0:T(8,128)(2,1)}, u32[]{:S(2)}) copy-start(bf16[32,64,256]{2,1,0:T(8,128)(2,1)} %param.11) | copy-start | bytes 3145732
  186.9 90.1 %copy-start.1 = (bf16[64,64,256]{2,1,0:T(8,128)(2,1)}, bf16[64,64,256]{2,1,0:T(8,128)(2,1)S(1)}, u32[]{:S(2)}) copy-start(bf16[64,64,256]{2,1,0:T(8,128)(2,1)S(1)} %scatter_fusion) | copy-start | bytes 6291460
  267.3 34.4 %all-to-all-start = ((bf16[8,8,1]{1,2,0:T(2,128)(2,1)}), bf16[8,8,1]{1,2,0:T(2,128)(2,1)S(1)}, u32[]{:S(2)}, u32[]{:S(2)}) async-start(bf16[8,8,1]{1,2,0:T(2,128)(2,1)} %all_to_all.132), calls=%async_computation | async-start | bytes 8192 | tf_op jit(solution)/shard_map/all_to_all | solution.py:147
  301.7 39.6 %all-to-all-start.1 = ((bf16[64,64,256]{2,1,0:T(8,128)(2,1)}), bf16[64,64,256]{2,1,0:T(8,128)(2,1)}, u32[]{:S(2)}, u32[]{:S(2)}) async-start(bf16[64,64,256]{2,1,0:T(8,128)(2,1)} %copy-done.1), calls=%async_computation.1 | async-start | bytes 4194304 | tf_op jit(solution)/shard_map/all_to_all | solution.py:144
  313.9 1.6 copy-start
  341.3 53.3 %all-to-all-start.5 = ((bf16[2,128,4096]{1,0,2:T(2,128)(2,1)}), bf16[2,128,4096]{1,0,2:T(2,128)(2,1)}, u32[]{:S(2)}, u32[]{:S(2)}) async-start(bf16[2,128,4096]{1,0,2:T(2,128)(2,1)} %copy.240), calls=%async_computation.5 | async-start | bytes 4194304 | tf_op jit(solution)/shard_map/all_to_all | solution.py:174
  345.8 1.2 copy-start.7
  348.6 1.3 copy-start.2
  349.9 49.8 %copy-start.10 = (bf16[32,2,256]{2,1,0:T(2,128)(2,1)S(1)}, bf16[32,2,256]{2,1,0:T(2,128)(2,1)}, u32[]{:S(2)}) copy-start(bf16[32,2,256]{2,1,0:T(2,128)(2,1)} %param.13) | copy-start | bytes 98308
  394.6 46.8 %all-to-all-start.6 = ((bf16[64,64,256]{2,1,0:T(8,128)(2,1)}), bf16[64,64,256]{2,1,0:T(8,128)(2,1)S(1)}, u32[]{:S(2)}, u32[]{:S(2)}) async-start(bf16[64,64,256]{2,1,0:T(8,128)(2,1)} %copy-done.2), calls=%async_computation.6 | async-start | bytes 4194304 | tf_op jit(solution)/shard_map/all_to_all | solution.py:145
  441.4 9.9 all-to-all-start.7
  478.3 52.3 %all-to-all-start.8 = ((bf16[2,512,1024]{2,0,1:T(2,128)(2,1)}), bf16[2,512,1024]{2,0,1:T(2,128)(2,1)S(1)}, u32[]{:S(2)}, u32[]{:S(2)}) async-start(bf16[2,512,1024]{2,0,1:T(2,128)(2,1)} %copy.245), calls=%async_computation.8 | async-start | bytes 4194304 | tf_op jit(solution)/shard_map/all_to_all | solution.py:202
  481.9 385.9 %all-gather.2.cloned.1.call-start = ((), (), s32[]{:S(2)}) async-start(), calls=%async_computation.14 | async-start | bytes 10485760 | tf_op jit(solution)/shard_map/all_gather | solution.py:228
  539.2 1.6 copy-start.5
  713.6 3.1 copy-start.3
  719.9 0.7 copy-start.13
  719.9 363.0 %reduce-scatter.2.cloned.1.call-start = ((), (), s32[]{:S(2)}) async-start(), calls=%async_computation.15 | async-start | bytes 10485760 | tf_op jit(solution)/shard_map/reduce_scatter | solution.py:230
  878.8 5.3 copy-start.9
  901.3 4.9 copy-start.8
  939.9 8.3 all-to-all-start.12
Sparse Core Ops, SparseCore 0:
  720.1 147.7 all-gather.1
  940.0 142.8 reduce-scatter.1
where the time goes:
time: 1110 us; the launch traced here: 1090 us
  waiting for transfers between devices  505 us (45%)
  local copies, waits for them, and re-layouts  205 us (18%)
  blocking collectives  160 us (14%)
  matrix products  126 us (11%)
  other arithmetic  42.6 us (4%)
  starting transfers between devices  39.7 us (4%)
  between operations  16 us (1%)
    all_gather x1, waiting for transfers between devices, shards(): gathered = lax.all_gather(estimate - gradient, 'wav', axis=1, tiled=True)  146 us
    reduce_scatter x1, waiting for transfers between devices, shards(): lax.psum_scatter(single, 'wav', scatter_dimension=1, tiled=True)  134 us
    all_to_all x1, waiting for transfers between devices, shards(): lax.all_to_all(lax.all_to_all(stacked, 'vis', split_axis=2, concat_axis=1...  80.4 us
    all_to_all x1, blocking collectives, shards(): lax.all_to_all(stacked, 'vis', split_axis=2, concat_axis=1, tiled=True)  51.6 us
    all_to_all x1, blocking collectives, shards(): lax.all_to_all(lax.all_to_all(stacked.astype(jnp.bfloat16), 'vis', split_...  51 us
    all_to_all x1, waiting for transfers between devices, shards(): lax.all_to_all(grid_grad.astype(jnp.bfloat16), 'wav', split_axis=1, conca...  48.5 us
    all_to_all x1, waiting for transfers between devices, shards(): lax.all_to_all(estimate, 'wav', split_axis=0, concat_axis=1, tiled=True)  47.7 us
    all_to_all x1, waiting for transfers between devices, shards(): lax.all_to_all(jnp.stack([real_part, imag_part], 0).astype(jnp.bfloat16),...  44.6 us
  transfers between devices with their start and end apart: 11, of which 7 were waited for; matrix products, arithmetic and copies ran while one was open for 12% of the time, Pallas kernels for 0%

commit v1 on v0

v1 whole, which is shorter than its diff:
```python
import math

import jax
import jax.numpy as jnp
import numpy as np
from jax import lax
from jax.sharding import PartitionSpec as P

PATCH = 64
HIGH = lax.Precision.HIGH
F32 = jnp.float32
BF16 = jnp.bfloat16
F16 = jnp.float16


def turns(rows, cols, period):
    angle = (rows * cols % period).astype(F32) * (2.0 * math.pi / period)
    return jnp.cos(angle), jnp.sin(angle)


def iota(size):
    return jnp.arange(size, dtype=jnp.int32)


def spread_matrix(groups, size):
    width = groups * size
    c = iota(width)
    return (c[:, None] == (c % size * groups + c // size)[None, :]).astype(F32)


def rows_forward(x, groups):
    rows = x.shape[1]
    count = groups * rows
    cos_g, sin_g = (np.cos(2 * np.pi * np.outer(np.arange(groups), np.arange(groups)) / groups), np.sin(2 * np.pi * np.outer(np.arange(groups), np.arange(groups)) / groups))
    mixed_re = jnp.einsum("kv,vnm->knm", jnp.asarray(cos_g, F32), x, precision=HIGH)
    mixed_im = -jnp.einsum("kv,vnm->knm", jnp.asarray(sin_g, F32), x, precision=HIGH)
    cos_t, sin_t = turns(iota(groups)[:, None], iota(rows)[None, :], count)
    cos_t, sin_t = cos_t[:, :, None], sin_t[:, :, None]
    both = jnp.concatenate([mixed_re * cos_t + mixed_im * sin_t, mixed_im * cos_t - mixed_re * sin_t], -1)
    cos_r, sin_r = turns(iota(rows)[:, None], iota(rows)[None, :], rows)
    p = jnp.einsum("kn,vnm->vkm", cos_r, both, precision=HIGH)
    q = jnp.einsum("kn,vnm->vkm", sin_r, both, precision=HIGH)
    m = x.shape[2]
    return jnp.concatenate([p[..., :m] + q[..., m:], p[..., m:] - q[..., :m]], -1)


def rows_inverse(y, groups):
    rows = y.shape[1]
    m = y.shape[2] // 2
    count = groups * rows
    cos_r, sin_r = turns(iota(rows)[:, None], iota(rows)[None, :], rows)
    p = jnp.einsum("kn,vnm->vkm", cos_r, y, precision=HIGH)
    q = jnp.einsum("kn,vnm->vkm", sin_r, y, precision=HIGH)
    re, im = p[..., :m] - q[..., m:], p[..., m:] + q[..., :m]
    cos_t, sin_t = turns(iota(groups)[:, None], iota(rows)[None, :], count)
    cos_t, sin_t = cos_t[:, :, None], sin_t[:, :, None]
    re, im = re * cos_t - im * sin_t, im * cos_t + re * sin_t
    cos_g, sin_g = (np.cos(2 * np.pi * np.outer(np.arange(groups), np.arange(groups)) / groups), np.sin(2 * np.pi * np.outer(np.arange(groups), np.arange(groups)) / groups))
    out = jnp.einsum("vk,knm->vnm", jnp.asarray(cos_g, F32), re, precision=HIGH)
    return out - jnp.einsum("vk,knm->vnm", jnp.asarray(sin_g, F32), im, precision=HIGH)


def column_matrix(wavs, m, down, scale):
    size = wavs * m
    cos_c, sin_c = turns(iota(size)[:, None], iota(size)[None, :], size)
    cos_c = (cos_c * scale).reshape(wavs, 1, m, down, 1, PATCH)
    sin_c = (sin_c * scale).reshape(wavs, 1, m, down, 1, PATCH)
    from_re = jnp.concatenate([cos_c, -sin_c], 4)
    from_im = jnp.concatenate([sin_c, cos_c], 4)
    return jnp.concatenate([from_re, from_im], 1).reshape(2 * size, 2 * size)


def soft(x, limit):
    return x - jnp.clip(x, -limit, limit)


def haar_mean(field, halo_left, halo_right, thresholds):
    bases = thresholds.shape[0]
    rows, width = field.shape
    pad = halo_left.shape[1]
    ext = jnp.concatenate([field, halo_right, halo_left], 1)
    span = ext.shape[1]
    place = iota(span)
    place = jnp.where(place < width + pad, place, place - span)
    root = math.sqrt(0.5)
    pairs = ext.reshape(rows // 2, 2, span)
    u = jnp.stack([(pairs[:, 0] + pairs[:, 1]) * root, (pairs[:, 0] - pairs[:, 1]) * root], 0)

    def limited(x, period):
        total = None
        for start in range(0, bases, period):
            index = place % period + start
            limit = jnp.zeros((span,), F32)
            inside = jnp.zeros((span,), jnp.bool_)
            for s in range(start, min(start + period, bases)):
                limit = jnp.where(index == s, thresholds[s], limit)
                inside = inside | (index == s)
            part = jnp.where(inside, soft(x, limit), 0.0)
            total = part if total is None else total + part
        return total

    def ahead(x, by):
        return jnp.roll(x, -by, axis=-1)

    def behind(x, by):
        return jnp.roll(x, by, axis=-1)

    s1 = (u + ahead(u, 1)) * root
    d1 = (u - ahead(u, 1)) * root
    s2 = (s1 + ahead(s1, 2)) * root
    d2 = (s1 - ahead(s1, 2)) * root
    s3 = (s2 + ahead(s2, 4)) * root
    d3 = (s2 - ahead(s2, 4)) * root
    s3, d3, d2, d1 = limited(s3, 8), limited(d3, 8), limited(d2, 4), limited(d1, 2)
    a2 = ((s3 + d3) + behind(s3 - d3, 4)) * root
    a1 = ((a2 + d2) + behind(a2 - d2, 2)) * root
    a0 = ((a1 + d1) + behind(a1 - d1, 1)) * root
    a0 = a0[..., :width] * (root / bases)
    return jnp.stack([a0[0] + a0[1], a0[0] - a0[1]], 1).reshape(rows, width)


def shards(image, kernel_v, kernel_u, measured, dest_owner, patch_slot, thresholds):
    vis = lax.axis_size("vis")
    wavs = lax.axis_size("wav")
    v = lax.axis_index("vis")
    rows, cols = image.shape
    img = rows * vis
    m = cols // vis
    down = rows // PATCH
    across = cols // PATCH
    blocks = kernel_v.shape[0]
    low = PATCH // vis
    spread = spread_matrix(vis, m)

    ids = jnp.concatenate([dest_owner, patch_slot[:, None]], 1)
    ids = lax.all_gather(ids, "vis", axis=0, tiled=True)
    owner, slot = ids[:, 0], ids[:, 1]
    a_block, b_block = slot // across, slot % across

    x = jnp.dot(image, spread, precision=HIGH).astype(F16)
    x = x.reshape(rows, vis, m).transpose(1, 0, 2)
    x = lax.all_to_all(x, "vis", split_axis=0, concat_axis=0, tiled=True).astype(F32)
    y = rows_forward(x, vis).astype(F16)
    y = y.reshape(vis, wavs, rows // wavs, 2 * m).transpose(1, 0, 2, 3)
    y = lax.all_to_all(y, "wav", split_axis=0, concat_axis=0, tiled=True).astype(F32)
    y = y.transpose(1, 2, 0, 3).reshape(cols, 2 * wavs * m)
    table = column_matrix(wavs, m, down, 1.0 / img)
    z = jnp.dot(y, table, precision=HIGH)
    z = z.reshape(vis, across, low, down, 2 * PATCH)
    tiles = z[:, b_block, :, a_block, :].reshape(vis * blocks, PATCH, 2 * PATCH)
    cos_k, sin_k = turns(v, owner[:, None] * rows + a_block[:, None] * PATCH + iota(PATCH)[None, :], img)
    cos_k = jnp.concatenate([cos_k, cos_k], 1)[:, None, :]
    sin_k = jnp.concatenate([sin_k, -sin_k], 1)[:, None, :]
    tiles = tiles * cos_k + jnp.roll(tiles, PATCH, axis=2) * sin_k
    tiles = lax.all_to_all(tiles.astype(F16), "vis", split_axis=0, concat_axis=0, tiled=True)
    patch = jnp.sum(tiles.reshape(vis, blocks, PATCH, 2 * PATCH).astype(F32), 0).astype(BF16)

    side_u = kernel_u.reshape(blocks, low, vis, -1).transpose(0, 2, 1, 3).reshape(kernel_u.shape)
    part_re = jnp.einsum("nba,nat->nbt", patch[..., :PATCH], kernel_v, preferred_element_type=F32)
    part_im = jnp.einsum("nba,nat->nbt", patch[..., PATCH:], kernel_v, preferred_element_type=F32)
    side = side_u.astype(F32)
    misfit = jnp.stack([jnp.sum(part_re * side, 1), jnp.sum(part_im * side, 1)], 1) - measured.astype(F32)
    w_re = (misfit[:, 0, None, :] * side).astype(BF16)
    w_im = (misfit[:, 1, None, :] * side).astype(BF16)
    term_re = jnp.einsum("nbt,nat->nba", w_re, kernel_v, preferred_element_type=F32)
    term_im = jnp.einsum("nbt,nat->nba", w_im, kernel_v, preferred_element_type=F32)
    terms = jnp.concatenate([term_re, term_im], -1).astype(BF16)

    terms = lax.all_gather(terms, "vis", axis=0, tiled=True).astype(F32)
    terms = terms * cos_k - jnp.roll(terms, PATCH, axis=2) * sin_k
    terms = terms.reshape(vis * blocks, vis, low, 2 * PATCH)
    flat = jnp.zeros((across * down, vis, low, 2 * PATCH), F32).at[b_block * down + a_block].add(terms)
    grad = flat.reshape(across, down, vis, low, 2 * PATCH).transpose(2, 0, 3, 1, 4).reshape(cols, 2 * rows)
    grad = lax.dot_general(grad, table, (((1,), (1,)), ((), ())), precision=HIGH).astype(BF16)
    grad = grad.reshape(cols, wavs, 2 * m).transpose(1, 0, 2)
    grad = lax.all_to_all(grad, "wav", split_axis=0, concat_axis=0, tiled=True).astype(F32)
    grad = grad.reshape(wavs, vis, rows // wavs, 2 * m).transpose(1, 0, 2, 3).reshape(vis, rows, 2 * m)
    grad = rows_inverse(grad, vis).astype(BF16)
    grad = lax.all_to_all(grad, "vis", split_axis=0, concat_axis=0, tiled=True)
    grad = grad.transpose(1, 0, 2).reshape(rows, cols)
    grad = lax.dot_general(grad, spread.astype(BF16), (((1,), (1,)), ((), ())), preferred_element_type=F32)
    shifted = image - grad
    halo = 8
    right = lax.ppermute(shifted[:, :halo], "wav", [(i, (i - 1) % wavs) for i in range(wavs)])
    left = lax.ppermute(shifted[:, -halo:], "wav", [(i, (i + 1) % wavs) for i in range(wavs)])
    return haar_mean(shifted, left, right, thresholds), misfit


def solution(mesh):
    both = ("vis", "wav")
    in_specs = (
        P("vis", "wav"),
        P(both, None, None),
        P(both, None, None),
        P(both, None, None),
        P(both, None),
        P(both),
        P(),
    )
    out_specs = (P("vis", "wav"), P(both, None, None))
    return jax.shard_map(shards, mesh=mesh, in_specs=in_specs, out_specs=out_specs, check_vma=False)
```

time: 1110 us -> 550 us (0.50); the launches traced: 1090 us -> 546 us
  waiting for transfers between devices: 505 us -> 131 us
  local copies, waits for them, and re-layouts: 205 us -> 95.3 us
  other arithmetic: 42.6 us -> 142 us
  blocking collectives: 160 us -> 62.1 us
  matrix products: 126 us -> 79.8 us
  starting transfers between devices: 39.7 us -> 20.6 us
    all_to_all x9 -> x4, waiting for transfers between devices: 225 us -> 84.7 us  [the longest x1 44.7 us: shards(): lax.all_to_all(tiles.astype(F16), 'vis', split_axis=0, concat_axis=0, til...]
    reduce_scatter x1 -> x0, waiting for transfers between devices: 134 us -> none  [shards(): lax.psum_scatter(single, 'wav', scatter_dimension=1, tiled=True)]
    all_gather x1, waiting for transfers between devices: 146 us -> 35 us  [shards(): terms = lax.all_gather(terms, 'vis', axis=0, tiled=True).astype(F32)]
    all_to_all x4 -> x1, blocking collectives: 160 us -> 53.2 us  [shards(): lax.all_to_all(grad, 'wav', split_axis=0, concat_axis=0, tiled=True)]
    convert_element_type x13 -> x1, local copies, waits for them, and re-layouts: 67.8 us -> 1.14 us  [shards(): grad = rows_inverse(grad, vis).astype(BF16)]
    dot_general x33 -> x16, matrix products: 126 us -> 79.8 us  [the longest x1 9.98 us: shards(): z = jnp.dot(y, table, precision=HIGH)]
    all_to_all x13 -> x1, local copies, waits for them, and re-layouts: 42.3 us -> 0.52 us  [shards(): grad = lax.all_to_all(grad, 'vis', split_axis=0, concat_axis=0, tiled=True)]
    scatter-add x0 -> x1, other arithmetic: none -> 39.8 us  [shards(): jnp.zeros((across * down, vis, low, 2 * PATCH), F32)]
  transfers between devices with their start and end apart: 11 -> 7, of which waited for: 7 -> 6; matrix products, arithmetic and copies ran while one was open for 12% -> 5% of each run, Pallas kernels for 0% -> 0%
where the time goes in v1:
time: 550 us; the launch traced here: 546 us
  other arithmetic  142 us (26%)
  waiting for transfers between devices  131 us (24%)
  local copies, waits for them, and re-layouts  95.3 us (17%)
  matrix products  79.8 us (15%)
  blocking collectives  62.1 us (11%)
  starting transfers between devices  20.6 us (4%)
  between operations  14.9 us (3%)
    all_to_all x1, blocking collectives, shards(): lax.all_to_all(grad, 'wav', split_axis=0, concat_axis=0, tiled=True)  53.2 us
    all_to_all x1, waiting for transfers between devices, shards(): lax.all_to_all(tiles.astype(F16), 'vis', split_axis=0, concat_axis=0, til...  44.7 us
    scatter-add x1, other arithmetic, shards(): jnp.zeros((across * down, vis, low, 2 * PATCH), F32)  39.8 us
    all_gather x1, waiting for transfers between devices, shards(): terms = lax.all_gather(terms, 'vis', axis=0, tiled=True).astype(F32)  35 us
    all_to_all x1, waiting for transfers between devices, shards(): lax.all_to_all(y, 'wav', split_axis=0, concat_axis=0, tiled=True)  21.8 us
    sub x1, other arithmetic, haar_mean(): a1 = (a2 + d2 + behind(a2 - d2, 2)) * root  13.8 us
    all_to_all x1, waiting for transfers between devices, shards(): lax.all_to_all(x, 'vis', split_axis=0, concat_axis=0, tiled=True)  13.4 us
    sub x1, other arithmetic, haar_mean(): a0 = (a1 + d1 + behind(a1 - d1, 1)) * root  12.6 us
  transfers between devices with their start and end apart: 7, of which 6 were waited for; matrix products, arithmetic and copies ran while one was open for 5% of the time, Pallas kernels for 0%

profile of v1, /device:TPU:2, one launch (start us, length us, event | category | flops | bytes accessed | tf_op | source)
XLA Modules:
  0.0 545.7 jit_solution(16483902062634614667)
XLA Ops:
  7.2 4.7 fusion.41
  13.5 4.6 all-to-all-start
  18.6 13.4 %all-to-all-done = f16[8,512,128]{2,1,0:T(8,128)(2,1)S(1)} async-done(((f16[8,512,128]{2,1,0:T(8,128)(2,1)}), f16[8,512,128]{2,1,0:T(8,128)(2,1)S(1)}, u32[]{:S(2)}, u32[]{:S(2)}) %all-to-all-start) | async-done | bytes 1048608 | tf_op jit(solution)/shard_map/all_to_all | solution.py:142
  33.4 5.1 fusion.25
  40.8 5.3 copy.105
  46.1 9.4 %convolution_bitcast_fusion = f32[8,512,256]{1,2,0:T(8,128)S(1)} fusion(f32[8,512,256]{1,2,0:T(8,128)} %copy.105), kind=kOutput, calls=%fused_computation.36 | convolution fusion | flops 3224895488 | bytes 8388608 | tf_op jit(solution)/shard_map/kn,vnm->vkm/dot_general | solution.py:42
  55.6 9.9 %convolution_bitcast_fusion.1 = f32[8,512,256]{1,2,0:T(8,128)S(1)} fusion(f32[8,512,256]{1,2,0:T(8,128)S(1)} %copy-done.3), kind=kOutput, calls=%fused_computation.37 | convolution fusion | flops 3224895488 | bytes 8388608 | tf_op jit(solution)/shard_map/kn,vnm->vkm/dot_general | solution.py:41
  69.1 5.0 all-to-all-start.1
  74.2 4.2 fusion.86
  79.1 5.2 copy.110
  84.4 6.5 %reshape.414 = f32[1024,1024]{0,1:T(8,128)} reshape(f32[4,2,128,8,2,64]{2,1,0,5,4,3:T(2,128)} %copy.110) | data formatting | bytes 8388608 | tf_op jit(solution)/shard_map/reshape | solution.py:70
  90.9 8.9 %all-gather = s32[8,32,2]{1,2,0:T(2,128)S(1)} all-gather(s32[1,32,2]{1,2,0:T(2,128)S(1)} %add_bitcast_fusion.1), channel_id=1, replica_groups=mesh['vis'=8,'wav'=4] {'vis'}, dimensions={0}, use_global_device_ids=true | all-gather | bytes 2304 | tf_op jit(solution)/shard_map/all_gather | solution.py:136
  100.7 21.8 %all-to-all-done.1 = f16[4,8,128,256]{2,3,1,0:T(8,128)(2,1)S(1)} async-done(((f16[4,8,128,256]{2,3,1,0:T(8,128)(2,1)}), f16[4,8,128,256]{2,3,1,0:T(8,128)(2,1)S(1)}, u32[]{:S(2)}, u32[]{:S(2)}) %all-to-all-start.1) | async-done | bytes 2097184 | tf_op jit(solution)/shard_map/all_to_all | solution.py:145
  122.5 3.1 copy.109
  125.6 3.5 reshape.448
  129.1 10.0 %fusion.23 = f32[8,16,8,8,128]{4,2,3,1,0:T(8,128)} fusion(f32[8,128,1024,1,1]{2,1,0,4,3:T(8,128)} %bitcast.164, f16[8,16,8,1024,1]{3,2,1,0,4:T(8,128)(2,1)S(1)} %reshape.448), kind=kOutput, calls=%fused_computation.61 | convolution fusion | flops 6442450944 | bytes 10485760 | tf_op jit(solution)/shard_map/dot_general | solution.py:148
  139.1 7.1 %gather_fusion = f32[256,8,8,128]{3,2,1,0:T(8,128)} fusion(f32[8,16,8,8,128]{4,2,3,1,0:T(8,128)} %fusion.23, s32[256]{0:T(256)S(1)} %bitcast.156), kind=kCustom, calls=%fused_computation | custom fusion | bytes 16779264 | tf_op jit(solution)/shard_map/gather | solution.py:150
  146.2 11.0 %fusion.145 = (f32[256,64,64]{2,1,0:T(8,128)S(1)}, f32[256,64,64]{2,1,0:T(8,128)}) fusion(f32[256,64,128]{2,1,0:T(8,128)} %bitcast.152), kind=kLoop, calls=%fused_computation.244 | loop fusion | bytes 16777216 | tf_op jit(solution)/shard_map/jit(_roll_static)/slice | solution.py:154
  157.3 7.2 %fusion.1 = f16[256,64,128]{2,1,0:T(8,128)(2,1)} fusion(f32[256,64,64]{2,1,0:T(8,128)} %get-tuple-element.23, f32[256,64,64]{2,1,0:T(8,128)S(1)} %get-tuple-element.22, f32[256,128]{1,0:T(8,128)S(1)} %get-tuple-element.61, f32[256,128]{1,0:T(8,128)S(1)} %get-tuple-element.60, f32[256,8,8,128]{3,2,1,0:T(8,128)S(1)} %bitcast.154), kind=kLoop, calls=%fused_computation.4 | loop fusion | flops 10485760 | bytes 21233664 | tf_op jit(solution)/shard_map/convert_element_type | solution.py:155
  164.5 4.5 all-to-all-start.2
  170.8 44.7 %all-to-all-done.2 = f16[256,64,128]{2,1,0:T(8,128)(2,1)} async-done(((f16[256,64,128]{2,1,0:T(8,128)(2,1)}), f16[256,64,128]{2,1,0:T(8,128)(2,1)}, u32[]{:S(2)}, u32[]{:S(2)}) %all-to-all-start.2) | async-done | bytes 4194336 | tf_op jit(solution)/shard_map/all_to_all | solution.py:155
  215.5 3.2 convert_reduce_fusion
  223.2 35.0 %all-gather.3.cloned.1.call-done = bf16[256,64,128]{2,1,0:T(8,128)(2,1)} async-done(((bf16[32,64,128]{2,1,0:T(8,128)(2,1)}), bf16[256,64,128]{2,1,0:T(8,128)(2,1)}) %all-gather.3.cloned.1.call-update) | async-done | bytes 4194320 | tf_op jit(solution)/shard_map/all_gather | solution.py:169
  258.1 10.9 %fusion.146 = (f32[256,64,64]{2,1,0:T(8,128)}, f32[256,64,64]{2,1,0:T(8,128)}) fusion(bf16[256,64,128]{2,1,0:T(8,128)(2,1)} %all-gather.3.cloned.1.call-done), kind=kLoop, calls=%fused_computation.245 | loop fusion | bytes 16777216 | tf_op jit(solution)/shard_map/jit(_roll_static)/slice | solution.py:170
  269.1 10.0 %fusion.3 = f32[256,8,8,128]{3,2,1,0:T(8,128)} fusion(f32[256,64,64]{2,1,0:T(8,128)} %get-tuple-element.29, f32[256,64,64]{2,1,0:T(8,128)} %get-tuple-element.28, f32[256,128]{1,0:T(8,128)S(1)} %get-tuple-element.61, f32[256,128]{1,0:T(8,128)S(1)} %get-tuple-element.60, bf16[256,64,128]{2,1,0:T(8,128)(2,1)S(1)} %copy-done.2), kind=kLoop, calls=%fused_computation.7 | loop fusion | flops 10485760 | bytes 21233664 | tf_op jit(solution)/shard_map/reshape | solution.py:171
  281.6 39.8 %scatter_fusion = f32[128,8,8,128]{3,2,1,0:T(8,128)} fusion(f32[128,8,8,128]{3,2,1,0:T(8,128)} %broadcast_in_dim.91, s32[256]{0:T(256)S(1)} %bitcast.176, f32[256,8,8,128]{3,2,1,0:T(8,128)} %fusion.3), kind=kCustom, calls=%fused_computation.1 | custom fusion | flops 2097152 | bytes 25166848 | tf_op jit(solution)/shard_map/scatter-add | solution.py:172
  321.5 4.8 copy.113
  326.3 7.5 %fusion.37 = bf16[1024,1024]{0,1:T(8,128)(2,1)S(1)} fusion(f32[1024,1024]{0,1:T(8,128)S(1)} %copy-done.4, f32[128,8,8,128]{3,2,1,0:T(8,128)S(1)} %bitcast.169), kind=kOutput, calls=%fused_computation.82 | convolution fusion | flops 6443499520 | bytes 10485760 | tf_op jit(solution)/shard_map/dot_general | solution.py:174
  333.8 53.2 %all_to_all.25 = bf16[4,1024,256]{1,2,0:T(8,128)(2,1)S(1)} all-to-all(bf16[4,1024,256]{1,2,0:T(8,128)(2,1)S(1)} %bitcast.170), channel_id=1, replica_groups=mesh['vis'=8,'wav'=4] {'wav'}, dimensions={0} | all-to-all | bytes 4194304 | tf_op jit(solution)/shard_map/all_to_all | solution.py:176
  391.4 8.9 %fusion.62 = f32[8,256,512]{2,1,0:T(8,128)} fusion(bf16[8,512,256]{1,2,0:T(8,128)(2,1)} %reshape.421), kind=kOutput, calls=%fused_computation.109 | convolution fusion | flops 3224895488 | bytes 6291456 | tf_op jit(solution)/shard_map/kn,vnm->vkm/dot_general | solution.py:52
  400.3 7.2 %fusion.59 = f32[8,256,512]{2,1,0:T(8,128)} fusion(bf16[8,512,256]{1,2,0:T(8,128)(2,1)S(1)} %copy-done.7), kind=kOutput, calls=%fused_computation.106 | convolution fusion | flops 3224895488 | bytes 6291456 | tf_op jit(solution)/shard_map/kn,vnm->vkm/dot_general | solution.py:53
  407.5 5.4 copy.115
  413.0 5.6 %copy.116 = f32[8,256,512]{1,0,2:T(8,128)} copy(f32[8,256,512]{2,1,0:T(8,128)} %fusion.59) | data formatting | bytes 8388608 | tf_op jit(solution)/shard_map/kn,vnm->vkm/dot_general | solution.py:53
  418.5 5.6 %fusion.27 = f32[512,128,8]{1,2,0:T(8,128)S(1)} fusion(f32[8,8,1]{1,0,2:T(8,128)S(1)} %copy-done.14, f32[8,512]{0,1:T(8,128)S(1)} %copy-done.11, f32[8,512]{0,1:T(8,128)S(1)} %copy-done.9, f32[8,512,256]{2,0,1:T(8,128)} %bitcast.167, f32[8,512,256]{2,0,1:T(8,128)} %bitcast.165), kind=kOutput, calls=%fused_computation.69 | convolution fusion | flops 27787264 | bytes 10518784 | tf_op jit(solution)/shard_map/vk,knm->vnm/dot_general | solution.py:60
  424.1 3.8 fusion.46
  429.1 4.0 all-to-all-start.4
  442.2 4.8 all-to-all-done.4
  447.5 2.9 fusion.40
  453.3 11.2 %collective-permute-done = f32[512,8]{1,0:T(8,128)S(1)} collective-permute-done((f32[512,8]{1,0:T(8,128)S(1)}, f32[512,8]{1,0:T(8,128)S(1)}, u32[]{:S(2)}, u32[]{:S(2)}) %collective-permute-start) | collective-permute-done | bytes 16416 | tf_op jit(solution)/shard_map/ppermute | solution.py:184
  464.5 2.9 concatenate.88
  469.9 5.3 multiply_bitcast_fusion
  475.2 5.8 %fusion.8 = f32[2,256,1039]{2,0,1:T(2,128)S(1)} fusion(f32[1,256,1040]{2,0,1:T(1,128)S(1)} %get-tuple-element.31, f32[1,256,1040]{2,0,1:T(1,128)S(1)} %get-tuple-element.30), kind=kLoop, calls=%fused_computation.22 | loop fusion | flops 531968 | bytes 4257792 | tf_op jit(solution)/shard_map/stack | solution.py:87
  481.2 3.5 add_multiply_fusion.1
  487.3 5.3 add_multiply_fusion
  495.2 6.9 %fusion.140 = f32[2,256,1040]{2,0,1:T(2,128)S(1)} fusion(f32[1040]{0:T(1024)S(1)} %get-tuple-element.54, f32[1040]{0:T(1024)S(1)} %get-tuple-element.52, f32[2,256,1040]{2,0,1:T(2,128)S(1)} %add_multiply_fusion, f32[2,256,4]{2,0,1:T(2,128)S(1)} %slice.231, f32[2,256,1036]{2,0,1:T(2,128)S(1)} %slice.230, pred[1040]{0:T(1024)(128)(4,1)S(1)} %get-tuple-element.63), kind=kLoop, calls=%fused_computation.241 | loop fusion | flops 7454720 | bytes 6399120 | tf_op jit(solution)/shard_map/sub | solution.py:115
  502.4 13.8 %fusion.141 = (f32[2,256,1040]{2,0,1:T(2,128)S(1)}, f32[2,256,1040]{2,0,1:T(2,128)S(1)}) fusion(f32[1040]{0:T(1024)S(1)} %get-tuple-element.55, f32[1040]{0:T(1024)S(1)} %get-tuple-element.51, f32[2,256,2]{2,0,1:T(2,128)S(1)} %slice.229, f32[2,256,1038]{2,0,1:T(2,128)S(1)} %slice.228, pred[1040]{0:T(1024)(128)(4,1)S(1)} %get-tuple-element.62, ...), kind=kLoop, calls=%fused_computation.242 | loop fusion | flops 15441920 | bytes 17058080 | tf_op jit(solution)/shard_map/sub | solution.py:116
  516.6 12.6 %fusion.142 = (f32[2,256,1040]{2,0,1:T(2,128)S(1)}, f32[2,256,1040]{2,0,1:T(2,128)S(1)}, f32[2,256,1040]{2,0,1:T(2,128)S(1)}) fusion(f32[1040]{0:T(1024)S(1)} %get-tuple-element.53, f32[1040]{0:T(1024)S(1)} %get-tuple-element.50, pred[1040]{0:T(1024)(128)(4,1)S(1)} %get-tuple-element.65, f32[1040]{0:T(1024)S(1)} %get-tuple-element.57, ...), kind=kLoop, calls=%fused_computation.243 | loop fusion | flops 14376960 | bytes 17067440 | tf_op jit(solution)/shard_map/sub | solution.py:117
  529.5 3.0 fusion.16
  (102 shorter events, 52.7 us)
Async XLA Ops:
  7.2 211.5 %copy-start = (bf16[32,64,256]{2,1,0:T(8,128)(2,1)S(1)}, bf16[32,64,256]{2,1,0:T(8,128)(2,1)}, u32[]{:S(2)}) copy-start(bf16[32,64,256]{2,1,0:T(8,128)(2,1)} %param.12) | copy-start | bytes 3145732
  11.9 20.0 %copy-start.14 = (f32[8,8,1]{1,0,2:T(8,128)S(1)}, f32[8,8,1]{1,0,2:T(8,128)}, u32[]{:S(2)}) copy-start(f32[8,8,1]{1,0,2:T(8,128)} %constant.223) | copy-start | bytes 772
  13.5 18.4 %all-to-all-start = ((f16[8,512,128]{2,1,0:T(8,128)(2,1)}), f16[8,512,128]{2,1,0:T(8,128)(2,1)S(1)}, u32[]{:S(2)}, u32[]{:S(2)}) async-start(f16[8,512,128]{2,1,0:T(8,128)(2,1)} %bitcast.6), calls=%async_computation | async-start | bytes 2097152 | tf_op jit(solution)/shard_map/all_to_all | solution.py:142
  18.1 15.3 %copy-start.17 = (f32[8,8,1]{1,0,2:T(8,128)S(1)}, f32[8,8,1]{1,0,2:T(8,128)}, u32[]{:S(2)}) copy-start(f32[8,8,1]{1,0,2:T(8,128)} %constant.222) | copy-start | bytes 772
  18.3 20.2 %copy-start.8 = (f32[8,512]{0,1:T(8,128)}, f32[8,512]{0,1:T(8,128)S(1)}, u32[]{:S(2)}) copy-start(f32[8,512]{0,1:T(8,128)S(1)} %copy.102) | copy-start | bytes 49156
  18.6 20.0 %copy-start.10 = (f32[8,512]{0,1:T(8,128)}, f32[8,512]{0,1:T(8,128)S(1)}, u32[]{:S(2)}) copy-start(f32[8,512]{0,1:T(8,128)S(1)} %copy.104) | copy-start | bytes 49156
  46.1 9.5 %copy-start.3 = (f32[8,512,256]{1,2,0:T(8,128)S(1)}, f32[8,512,256]{1,2,0:T(8,128)}, u32[]{:S(2)}) copy-start(f32[8,512,256]{1,2,0:T(8,128)} %copy.105) | copy-start | bytes 12582916
  69.1 53.4 %all-to-all-start.1 = ((f16[4,8,128,256]{2,3,1,0:T(8,128)(2,1)}), f16[4,8,128,256]{2,3,1,0:T(8,128)(2,1)S(1)}, u32[]{:S(2)}, u32[]{:S(2)}) async-start(f16[4,8,128,256]{2,3,1,0:T(8,128)(2,1)} %maximum_bitcast_fusion), calls=%async_computation.1 | async-start | bytes 4194304 | tf_op jit(solution)/shard_map/all_to_all | solution.py:145
  84.3 6.5 %copy-start.15 = (s32[32]{0:T(128)S(1)}, s32[32]{0:T(128)}, u32[]{:S(2)}) copy-start(s32[32]{0:T(128)} %param.16) | copy-start | bytes 388
  84.3 6.5 %copy-start.16 = (s32[32,1]{0,1:T(1,128)S(1)}, s32[32,1]{0,1:T(1,128)}, u32[]{:S(2)}) copy-start(s32[32,1]{0,1:T(1,128)} %param.15) | copy-start | bytes 388
  146.2 11.1 %slice-start = ((s8[8388608]{0:T(1024)(128)(4,1)}), s8[4194304]{0:T(1024)(128)(4,1)S(1)}, s32[]{:S(2)}) async-start(s8[8388608]{0:T(1024)(128)(4,1)} %bitcast.153), calls=%async_computation.6 | async-start | bytes 8388608
  146.2 11.1 %slice-start.1 = ((s8[8388608]{0:T(1024)(128)(4,1)}), s8[4194304]{0:T(1024)(128)(4,1)S(1)}, s32[]{:S(2)}) async-start(s8[8388608]{0:T(1024)(128)(4,1)} %bitcast.153), calls=%async_computation.7 | async-start | bytes 8388608
  164.5 51.0 %all-to-all-start.2 = ((f16[256,64,128]{2,1,0:T(8,128)(2,1)}), f16[256,64,128]{2,1,0:T(8,128)(2,1)}, u32[]{:S(2)}, u32[]{:S(2)}) async-start(f16[256,64,128]{2,1,0:T(8,128)(2,1)} %fusion.1), calls=%async_computation.2 | async-start | bytes 8388608 | tf_op jit(solution)/shard_map/all_to_all | solution.py:155
  169.0 89.1 %all-gather.3.cloned.1.call-start = ((), (), s32[]{:S(2)}) async-start(), calls=%async_computation.5 | async-start | bytes 4718592 | tf_op jit(solution)/shard_map/all_gather | solution.py:169
  219.5 1.0 copy-start.12
  258.1 11.0 %copy-start.2 = (bf16[256,64,128]{2,1,0:T(8,128)(2,1)S(1)}, bf16[256,64,128]{2,1,0:T(8,128)(2,1)}, u32[]{:S(2)}) copy-start(bf16[256,64,128]{2,1,0:T(8,128)(2,1)} %all-gather.3.cloned.1.call-done) | copy-start | bytes 12582916
  321.5 4.8 copy-start.4
  391.4 8.9 %copy-start.7 = (bf16[8,512,256]{1,2,0:T(8,128)(2,1)S(1)}, bf16[8,512,256]{1,2,0:T(8,128)(2,1)}, u32[]{:S(2)}) copy-start(bf16[8,512,256]{1,2,0:T(8,128)(2,1)} %reshape.421) | copy-start | bytes 6291460
  413.0 5.6 %copy-start.9 = (f32[8,512]{0,1:T(8,128)S(1)}, f32[8,512]{0,1:T(8,128)}, u32[]{:S(2)}) copy-start(f32[8,512]{0,1:T(8,128)} %copy-done.8) | copy-start | bytes 49156
  413.0 5.6 %copy-start.11 = (f32[8,512]{0,1:T(8,128)S(1)}, f32[8,512]{0,1:T(8,128)}, u32[]{:S(2)}) copy-start(f32[8,512]{0,1:T(8,128)} %copy-done.10) | copy-start | bytes 49156
  418.5 5.6 %copy-start.5 = (f32[8,256,512]{1,0,2:T(8,128)S(1)}, f32[8,256,512]{1,0,2:T(8,128)}, u32[]{:S(2)}) copy-start(f32[8,256,512]{1,0,2:T(8,128)} %copy.115) | copy-start | bytes 12582916
  427.9 5.2 copy-start.13
  429.1 17.9 %all-to-all-start.4 = ((bf16[8,512,128]{2,1,0:T(8,128)(2,1)}), bf16[8,512,128]{2,1,0:T(8,128)(2,1)S(1)}, u32[]{:S(2)}, u32[]{:S(2)}) async-start(bf16[8,512,128]{2,1,0:T(8,128)(2,1)} %copy.117), calls=%async_computation.4 | async-start | bytes 2097152 | tf_op jit(solution)/shard_map/all_to_all | solution.py:179
  450.4 14.1 %copy-start.6 = (f32[512,1024]{1,0:T(8,128)}, f32[512,1024]{1,0:T(8,128)S(1)}, u32[]{:S(2)}) copy-start(f32[512,1024]{1,0:T(8,128)S(1)} %fusion.40) | copy-start | bytes 6291460
  450.6 13.9 %collective-permute-start = (f32[512,8]{1,0:T(8,128)S(1)}, f32[512,8]{1,0:T(8,128)S(1)}, u32[]{:S(2)}, u32[]{:S(2)}) collective-permute-start(f32[512,8]{1,0:T(8,128)S(1)} %get-tuple-element.35), channel_id=1, source_target_pairs={{0,3},{1,0},{2,1},{3,2},{4,7},{5,4},{6,5},{7,6},{8,11},{9,8},{10,9... | collective-permute-start | bytes 49160 | tf_op jit(solution)/shard_map/ppermute | solution.py:184
  452.1 12.5 %collective-permute-start.1 = (f32[512,8]{1,0:T(8,128)S(1)}, f32[512,8]{1,0:T(8,128)S(1)}, u32[]{:S(2)}, u32[]{:S(2)}) collective-permute-start(f32[512,8]{1,0:T(8,128)S(1)} %get-tuple-element.34), channel_id=1, source_target_pairs={{0,1},{1,2},{2,3},{3,0},{4,5},{5,6},{6,7},{7,4},{8,9},{9,10},{10,1... | collective-permute-start | bytes 49160 | tf_op jit(solution)/shard_map/ppermute | solution.py:185
  534.3 4.4 copy-start.1
Sparse Core Ops, SparseCore 0:
  223.3 34.7 all-gather.2

commit v2 on v1

--- a/solution.py
+++ b/solution.py
@@ -4,6 +4,8 @@
 import jax.numpy as jnp
 import numpy as np
 from jax import lax
+from jax.experimental import pallas as pl
+from jax.experimental.pallas import tpu as pltpu
 from jax.sharding import PartitionSpec as P
 
 PATCH = 64
@@ -70,53 +72,316 @@
     return jnp.concatenate([from_re, from_im], 1).reshape(2 * size, 2 * size)
 
 
-def soft(x, limit):
-    return x - jnp.clip(x, -limit, limit)
+def split(x):
+    high = lax.reduce_precision(x, 8, 7)
+    return high.astype(BF16), (x - high).astype(BF16)
+
+
+def cosine(count, period):
+    part = (count % period).astype(F32) * (1.0 / period)
+    part = 0.25 - jnp.abs(part - jnp.round(part))
+    square = part * part
+    terms = [(-1) ** i * (2 * math.pi) ** (2 * i + 1) / math.factorial(2 * i + 1) for i in range(7)]
+    value = jnp.full_like(part, terms[-1])
+    for term in terms[-2::-1]:
+        value = value * square + term
+    return value * part
+
+
+def row_table(size):
+    k, n = lax.broadcasted_iota(jnp.int32, (2 * size, size), 0), lax.broadcasted_iota(jnp.int32, (2 * size, size), 1)
+    return split(cosine(k % size * n - k // size * (size // 4), size))
+
+
+def column_table(wavs, m, turned):
+    size = wavs * m
+    shape = (2 * size, 2 * size)
+    row, col = lax.broadcasted_iota(jnp.int32, shape, int(turned)), lax.broadcasted_iota(jnp.int32, shape, 1 - int(turned))
+    n = row // (2 * m) * m + row % m
+    k = col // (2 * PATCH) * PATCH + col % PATCH
+    quarter = col // PATCH % 2 - row // m % 2
+    return split(cosine(n * k + quarter * (size // 4), size))
+
+
+def twist_table(groups, rows):
+    n, k = lax.broadcasted_iota(jnp.int32, (rows, 2 * groups), 0), lax.broadcasted_iota(jnp.int32, (rows, 2 * groups), 1)
+    count = groups * rows
+    return cosine(n * (k % groups) - k // groups * (count // 4), count)
+
+
+def in_vmem(count):
+    return [pl.BlockSpec(memory_space=pltpu.VMEM)] * count
+
+
+VMEM_LIMIT = 56 * 1024 * 1024
+ROOT = math.sqrt(0.5)
+
+
+def rows_forward_kernel(x_ref, high_ref, low_ref, twist_ref, y_ref):
+    rows, m = x_ref.shape[1:]
+    wavs = y_ref.shape[0]
+    part = rows // wavs
+    x = [x_ref[i] for i in range(8)]
+    e0, e1, f0, f1 = x[0] + x[4], x[0] - x[4], x[2] + x[6], x[2] - x[6]
+    g0, g1, h0, h1 = x[1] + x[5], x[1] - x[5], x[3] + x[7], x[3] - x[7]
+    gm, gp = (g1 - h1) * ROOT, (g1 + h1) * ROOT
+    zero = jnp.zeros_like(e0)
+    mixed = (
+        (e0 + f0 + g0 + h0, zero),
+        (e1 + gm, -f1 - gp),
+        (e0 - f0, h0 - g0),
+        (e1 - gm, f1 - gp),
+        (e0 + f0 - g0 - h0, zero),
+    )
+    for k, (re, im) in enumerate(mixed):
+        if k:
+            cos_t, sin_t = twist_ref[:, k : k + 1], twist_ref[:, 8 + k : 9 + k]
+            re, im = re * cos_t + im * sin_t, im * cos_t - re * sin_t
+        both = jnp.concatenate([re, im], 1)
+        high = both.astype(BF16)
+        low = (both - high.astype(F32)).astype(BF16)
+        out = jnp.dot(high_ref[...], high, preferred_element_type=F32)
+        out += jnp.dot(high_ref[...], low, preferred_element_type=F32)
+        out += jnp.dot(low_ref[...], high, preferred_element_type=F32)
+        p_re, p_im, q_re, q_im = out[:rows, :m], out[:rows, m:], out[rows:, :m], out[rows:, m:]
+        here = jnp.concatenate([p_re + q_im, p_im - q_re], 1)
+        for w in range(wavs):
+            y_ref[w, k] = here[w * part : (w + 1) * part]
+        if k in (1, 2, 3):
+            there = jnp.concatenate([p_re - q_im, -p_im - q_re], 1)
+            there = pltpu.roll(there, rows - 1, 0)
+            for w in range(wavs):
+                y_ref[w, 8 - k] = there[w * part : (w + 1) * part]
+
+
+def rows_forward_fast(x, wavs, table, twist):
+    groups, rows, m = x.shape
+    return pl.pallas_call(
+        rows_forward_kernel,
+        in_specs=in_vmem(4),
+        out_specs=in_vmem(1)[0],
+        out_shape=jax.ShapeDtypeStruct((wavs, groups, rows // wavs, 2 * m), F32),
+        compiler_params=pltpu.CompilerParams(vmem_limit_bytes=VMEM_LIMIT),
+        name="rows_forward",
+    )(x, *table, twist)
+
+
+AT_ONCE = 8
+
+
+def shares_kernel(a_ref, b_ref, y_ref, high_ref, low_ref, cos_ref, sin_ref, tile_ref, z_ref, head_ref, rest_ref):
+    wavs, groups, part, double = y_ref.shape
+    down = z_ref.shape[0]
+    count, low = tile_ref.shape[0], PATCH // groups
+    wide = 2 * PATCH
+    scale = 1.0 / (groups * down * PATCH)
+    for k in range(groups):
+        for w in range(wavs):
+            y = y_ref[w, k]
+            high = y.astype(BF16)
+            spot = (pl.ds(k * part, part), pl.ds(w * double, double))
+            head_ref[spot] = high
+            rest_ref[spot] = (y - high.astype(F32)).astype(BF16)
+    for a in range(0, down, 2):
+        spot = (slice(None), pl.ds(a * wide, 2 * wide))
+        z = jnp.dot(head_ref[...], high_ref[spot], preferred_element_type=F32)
+        z += jnp.dot(rest_ref[...], high_ref[spot], preferred_element_type=F32)
+        z += jnp.dot(head_ref[...], low_ref[spot], preferred_element_type=F32)
+        z = z * scale
+        z_ref[a] = z[:, :wide].reshape(groups, part, wide)
+        z_ref[a + 1] = z[:, wide:].reshape(groups, part, wide)
+
+    @pl.loop(0, count // AT_ONCE)
+    def _(step):
+        for i in range(AT_ONCE):
+            n = step * AT_ONCE + i
+            start = pl.multiple_of(b_ref[n] * low, low)
+            tile = z_ref[a_ref[n], :, pl.ds(start, low), :].reshape(PATCH, wide)
+            tile_ref[n] = tile * cos_ref[pl.ds(n, 1), :] + pltpu.roll(tile, PATCH, 1) * sin_ref[pl.ds(n, 1), :]
+
+
+def shares_fast(a_block, b_block, y, table, cos_k, sin_k):
+    wavs, groups, part, double = y.shape
+    down = wavs * double // 2 // PATCH
+    return pl.pallas_call(
+        shares_kernel,
+        in_specs=[pl.BlockSpec(memory_space=pltpu.SMEM)] * 2 + in_vmem(5),
+        out_specs=in_vmem(1)[0],
+        out_shape=jax.ShapeDtypeStruct((a_block.shape[0], PATCH, 2 * PATCH), F32),
+        scratch_shapes=[pltpu.VMEM((down, groups, part, 2 * PATCH), F32)] + [pltpu.VMEM((groups * part, wavs * double), BF16)] * 2,
+        compiler_params=pltpu.CompilerParams(vmem_limit_bytes=VMEM_LIMIT),
+        name="shares",
+    )(a_block, b_block, y, *table, cos_k, sin_k)
+
+
+def gather_kernel(a_ref, b_ref, term_ref, high_ref, low_ref, cos_ref, sin_ref, y_ref, g_ref, head_ref):
+    wavs, groups, part, double = y_ref.shape
+    down = g_ref.shape[0]
+    count, low = term_ref.shape[0], PATCH // groups
+    wide = 2 * PATCH
+    g_ref[...] = jnp.zeros_like(g_ref)
+
+    @pl.loop(0, count // AT_ONCE)
+    def _(step):
+        tiles = []
+        for i in range(AT_ONCE):
+            n = step * AT_ONCE + i
+            tile = term_ref[n].astype(F32)
+            tiles.append(tile * cos_ref[pl.ds(n, 1), :] - pltpu.roll(tile, PATCH, 1) * sin_ref[pl.ds(n, 1), :])
+        for i in range(AT_ONCE):
+            n = step * AT_ONCE + i
+            start = pl.multiple_of(b_ref[n] * low, low)
+            g_ref[a_ref[n], :, pl.ds(start, low), :] += tiles[i].reshape(groups, low, wide)
+
+    for a in range(down):
+        head_ref[:, a * wide : (a + 1) * wide] = g_ref[a].reshape(groups * part, wide).astype(BF16)
+    scale = 1.0 / (groups * down * PATCH)
+    for w in range(wavs):
+        spot = (slice(None), pl.ds(w * double, double))
+        y = jnp.dot(head_ref[...], high_ref[spot], preferred_element_type=F32)
+        y += jnp.dot(head_ref[...], low_ref[spot], preferred_element_type=F32)
+        y_ref[w] = (y * scale).astype(BF16).reshape(groups, part, double)
+
+
+def gather_fast(a_block, b_block, terms, table, cos_k, sin_k, wavs, groups, part, m):
+    down = wavs * m // PATCH
+    return pl.pallas_call(
+        gather_kernel,
+        in_specs=[pl.BlockSpec(memory_space=pltpu.SMEM)] * 2 + in_vmem(5),
+        out_specs=in_vmem(1)[0],
+        out_shape=jax.ShapeDtypeStruct((wavs, groups, part, 2 * m), BF16),
+        scratch_shapes=[pltpu.VMEM((down, groups, part, 2 * PATCH), F32), pltpu.VMEM((groups * part, 2 * PATCH * down), BF16)],
+        compiler_params=pltpu.CompilerParams(vmem_limit_bytes=VMEM_LIMIT),
+        name="gather",
+    )(a_block, b_block, terms, *table, cos_k, sin_k)
+
+
+def rows_inverse_kernel(y_ref, high_ref, low_ref, twist_ref, x_ref, re_ref, im_ref):
+    rows, m = x_ref.shape[1:]
+    wavs = y_ref.shape[0]
+    for k in range(8):
+        y = jnp.concatenate([y_ref[w, k] for w in range(wavs)], 0)
+        out = jnp.dot(high_ref[...], y, preferred_element_type=F32)
+        out += jnp.dot(low_ref[...], y, preferred_element_type=F32)
+        re, im = out[:rows, :m] - out[rows:, m:], out[:rows, m:] + out[rows:, :m]
+        if k:
+            cos_t, sin_t = twist_ref[:, k : k + 1], twist_ref[:, 8 + k : 9 + k]
+            re, im = re * cos_t - im * sin_t, im * cos_t + re * sin_t
+        re_ref[k] = re
+        im_ref[k] = im
+    even, odd = re_ref[0] + re_ref[4], re_ref[0] - re_ref[4]
+    r1, r2, r3 = re_ref[1] + re_ref[7], re_ref[2] + re_ref[6], re_ref[3] + re_ref[5]
+    i1, i2, i3 = im_ref[1] - im_ref[7], im_ref[2] - im_ref[6], im_ref[3] - im_ref[5]
+    rm, ip = (r1 - r3) * ROOT, (i1 + i3) * ROOT
+    x_ref[0] = (even + r2 + (r1 + r3)).astype(BF16)
+    x_ref[4] = (even + r2 - (r1 + r3)).astype(BF16)
+    x_ref[2] = (even - r2 - (i1 - i3)).astype(BF16)
+    x_ref[6] = (even - r2 + (i1 - i3)).astype(BF16)
+    x_ref[1] = (odd + rm - ip - i2).astype(BF16)
+    x_ref[7] = (odd + rm + ip + i2).astype(BF16)
+    x_ref[3] = (odd - rm - ip + i2).astype(BF16)
+    x_ref[5] = (odd - rm + ip - i2).astype(BF16)
+
+
+def rows_inverse_fast(y, table, twist):
+    wavs, groups, part, double = y.shape
+    rows, m = wavs * part, double // 2
+    return pl.pallas_call(
+        rows_inverse_kernel,
+        in_specs=in_vmem(4),
+        out_specs=in_vmem(1)[0],
+        out_shape=jax.ShapeDtypeStruct((groups, rows, m), BF16),
+        scratch_shapes=[pltpu.VMEM((groups, rows, m), F32)] * 2,
+        compiler_params=pltpu.CompilerParams(vmem_limit_bytes=VMEM_LIMIT),
+        name="rows_inverse",
+    )(y, *table, twist)
+
+
+HALO = 8
+LANES = 128
+
+
+def haar_kernel(field_ref, edge_ref, limit_ref, out_ref, *, bases):
+    rows, width = field_ref.shape
+    span = width + LANES
+    even = lax.broadcasted_iota(jnp.int32, (rows, span), 0) % 2 == 0
+
+    def mix(x, even):
+        other = jnp.where(even, pltpu.roll(x, rows - 1, 0), pltpu.roll(x, 1, 0))
+        return jnp.where(even, x, -x) + other
+
+    def ahead(x, by):
+        return pltpu.roll(x, span - by, 1)
+
+    def behind(x, by):
+        return pltpu.roll(x, by, 1)
+
+    def mean(u):
+        spot = 0
+        level = []
+        for period in (2, 4, 8):
+            forward = ahead(u, period // 2)
+            parts = [u + forward, u - forward]
+            limits = []
+            for start in range(0, bases, period):
+                limits.append(limit_ref[spot : spot + 1, :])
+                spot += 1
+            limited = []
+            for x in parts if period == 8 else parts[1:]:
+                total = None
+                for limit in limits:
+                    x_soft = x - jnp.minimum(jnp.maximum(x, -limit), limit)
+                    total = x_soft if total is None else total + x_soft
+                limited.append(total)
+            level.append(limited)
+            u = parts[0]
+        s3, d3 = level[2]
+        back = (s3 + d3) + behind(s3 - d3, 4)
+        for by, (d,) in ((2, level[1]), (1, level[0])):
+            back = back * 0.5
+            back = (back + d) + behind(back - d, by)
+        return back[:, :width] * (0.25 / bases)
+
+    field = jnp.concatenate([field_ref[...], edge_ref[...]], 1)
+    out_ref[...] = mix(mean(mix(field, even)), even[:, :width])
+
+
+def haar_limits(width, thresholds):
+    bases = thresholds.shape[0]
+    span = width + LANES
+    place = iota(span)
+    place = jnp.where(place < width + LANES // 2, place, place - span) + 8
+    out = []
+    for period in (2, 4, 8):
+        scale = math.sqrt(2.0 * period)
+        for start in range(0, bases, period):
+            index = place % period + start
+            limit = jnp.full((span,), 3e38, F32)
+            for s in range(start, min(start + period, bases)):
+                limit = jnp.where(index == s, thresholds[s] * scale, limit)
+            out.append(limit)
+    return jnp.stack(out)
 
 
 def haar_mean(field, halo_left, halo_right, thresholds):
     bases = thresholds.shape[0]
     rows, width = field.shape
-    pad = halo_left.shape[1]
-    ext = jnp.concatenate([field, halo_right, halo_left], 1)
-    span = ext.shape[1]
-    place = iota(span)
-    place = jnp.where(place < width + pad, place, place - span)
-    root = math.sqrt(0.5)
-    pairs = ext.reshape(rows // 2, 2, span)
-    u = jnp.stack([(pairs[:, 0] + pairs[:, 1]) * root, (pairs[:, 0] - pairs[:, 1]) * root], 0)
-
-    def limited(x, period):
-        total = None
-        for start in range(0, bases, period):
-            index = place % period + start
-            limit = jnp.zeros((span,), F32)
-            inside = jnp.zeros((span,), jnp.bool_)
-            for s in range(start, min(start + period, bases)):
-                limit = jnp.where(index == s, thresholds[s], limit)
-                inside = inside | (index == s)
-            part = jnp.where(inside, soft(x, limit), 0.0)
-            total = part if total is None else total + part
-        return total
-
-    def ahead(x, by):
-        return jnp.roll(x, -by, axis=-1)
-
-    def behind(x, by):
-        return jnp.roll(x, by, axis=-1)
-
-    s1 = (u + ahead(u, 1)) * root
-    d1 = (u - ahead(u, 1)) * root
-    s2 = (s1 + ahead(s1, 2)) * root
-    d2 = (s1 - ahead(s1, 2)) * root
-    s3 = (s2 + ahead(s2, 4)) * root
-    d3 = (s2 - ahead(s2, 4)) * root
-    s3, d3, d2, d1 = limited(s3, 8), limited(d3, 8), limited(d2, 4), limited(d1, 2)
-    a2 = ((s3 + d3) + behind(s3 - d3, 4)) * root
-    a1 = ((a2 + d2) + behind(a2 - d2, 2)) * root
-    a0 = ((a1 + d1) + behind(a1 - d1, 1)) * root
-    a0 = a0[..., :width] * (root / bases)
-    return jnp.stack([a0[0] + a0[1], a0[0] - a0[1]], 1).reshape(rows, width)
+    middle = jnp.zeros((rows, LANES - 2 * HALO), F32)
+    edge = jnp.concatenate([halo_right, middle, halo_left], 1)
+    limits = haar_limits(width, thresholds)
+    step = min(rows, 64)
+    return pl.pallas_call(
+        lambda *refs: haar_kernel(*refs, bases=bases),
+        grid=(rows // step,),
+        in_specs=[
+            pl.BlockSpec((step, width), lambda i: (i, 0)),
+            pl.BlockSpec((step, LANES), lambda i: (i, 0)),
+            pl.BlockSpec(limits.shape, lambda i: (0, 0)),
+        ],
+        out_specs=pl.BlockSpec((step, width), lambda i: (i, 0)),
+        out_shape=jax.ShapeDtypeStruct((rows, width), F32),
+        name="haar",
+    )(field, edge, limits)
 
 
 def shards(image, kernel_v, kernel_u, measured, dest_owner, patch_slot, thresholds):
@@ -130,6 +395,8 @@
     across = cols // PATCH
     blocks = kernel_v.shape[0]
     low = PATCH // vis
+    part = rows // wavs
+    fast = vis == 8 and m == LANES and low == 8 and part % 8 == 0
     spread = spread_matrix(vis, m)
 
     ids = jnp.concatenate([dest_owner, patch_slot[:, None]], 1)
@@ -140,18 +407,25 @@
     x = jnp.dot(image, spread, precision=HIGH).astype(F16)
     x = x.reshape(rows, vis, m).transpose(1, 0, 2)
     x = lax.all_to_all(x, "vis", split_axis=0, concat_axis=0, tiled=True).astype(F32)
-    y = rows_forward(x, vis).astype(F16)
-    y = y.reshape(vis, wavs, rows // wavs, 2 * m).transpose(1, 0, 2, 3)
+    if fast:
+        rows_high_low, twist = row_table(rows), twist_table(vis, rows)
+        y = rows_forward_fast(x, wavs, rows_high_low, twist).astype(F16)
+    else:
+        y = rows_forward(x, vis).astype(F16)
+        y = y.reshape(vis, wavs, part, 2 * m).transpose(1, 0, 2, 3)
     y = lax.all_to_all(y, "wav", split_axis=0, concat_axis=0, tiled=True).astype(F32)
-    y = y.transpose(1, 2, 0, 3).reshape(cols, 2 * wavs * m)
-    table = column_matrix(wavs, m, down, 1.0 / img)
-    z = jnp.dot(y, table, precision=HIGH)
-    z = z.reshape(vis, across, low, down, 2 * PATCH)
-    tiles = z[:, b_block, :, a_block, :].reshape(vis * blocks, PATCH, 2 * PATCH)
     cos_k, sin_k = turns(v, owner[:, None] * rows + a_block[:, None] * PATCH + iota(PATCH)[None, :], img)
-    cos_k = jnp.concatenate([cos_k, cos_k], 1)[:, None, :]
-    sin_k = jnp.concatenate([sin_k, -sin_k], 1)[:, None, :]
-    tiles = tiles * cos_k + jnp.roll(tiles, PATCH, axis=2) * sin_k
+    cos_k = jnp.concatenate([cos_k, cos_k], 1)
+    sin_k = jnp.concatenate([sin_k, -sin_k], 1)
+    if fast:
+        tiles = shares_fast(a_block, b_block, y, column_table(wavs, m, False), cos_k, sin_k)
+    else:
+        y = y.transpose(1, 2, 0, 3).reshape(cols, 2 * wavs * m)
+        table = column_matrix(wavs, m, down, 1.0 / img)
+        z = jnp.dot(y, table, precision=HIGH)
+        z = z.reshape(vis, across, low, down, 2 * PATCH)
+        tiles = z[:, b_block, :, a_block, :].reshape(vis * blocks, PATCH, 2 * PATCH)
+        tiles = tiles * cos_k[:, None] + jnp.roll(tiles, PATCH, axis=2) * sin_k[:, None]
     tiles = lax.all_to_all(tiles.astype(F16), "vis", split_axis=0, concat_axis=0, tiled=True)
     patch = jnp.sum(tiles.reshape(vis, blocks, PATCH, 2 * PATCH).astype(F32), 0).astype(BF16)
 
@@ -166,23 +440,29 @@
     term_im = jnp.einsum("nbt,nat->nba", w_im, kernel_v, preferred_element_type=F32)
     terms = jnp.concatenate([term_re, term_im], -1).astype(BF16)
 
-    terms = lax.all_gather(terms, "vis", axis=0, tiled=True).astype(F32)
-    terms = terms * cos_k - jnp.roll(terms, PATCH, axis=2) * sin_k
-    terms = terms.reshape(vis * blocks, vis, low, 2 * PATCH)
-    flat = jnp.zeros((across * down, vis, low, 2 * PATCH), F32).at[b_block * down + a_block].add(terms)
-    grad = flat.reshape(across, down, vis, low, 2 * PATCH).transpose(2, 0, 3, 1, 4).reshape(cols, 2 * rows)
-    grad = lax.dot_general(grad, table, (((1,), (1,)), ((), ())), precision=HIGH).astype(BF16)
-    grad = grad.reshape(cols, wavs, 2 * m).transpose(1, 0, 2)
-    grad = lax.all_to_all(grad, "wav", split_axis=0, concat_axis=0, tiled=True).astype(F32)
-    grad = grad.reshape(wavs, vis, rows // wavs, 2 * m).transpose(1, 0, 2, 3).reshape(vis, rows, 2 * m)
-    grad = rows_inverse(grad, vis).astype(BF16)
+    terms = lax.all_gather(terms, "vis", axis=0, tiled=True)
+    if fast:
+        grad = gather_fast(a_block, b_block, terms, column_table(wavs, m, True), cos_k, sin_k, wavs, vis, part, m)
+    else:
+        terms = terms.astype(F32)
+        terms = terms * cos_k[:, None] - jnp.roll(terms, PATCH, axis=2) * sin_k[:, None]
+        terms = terms.reshape(vis * blocks, vis, low, 2 * PATCH)
+        flat = jnp.zeros((across * down, vis, low, 2 * PATCH), F32).at[b_block * down + a_block].add(terms)
+        grad = flat.reshape(across, down, vis, low, 2 * PATCH).transpose(2, 0, 3, 1, 4).reshape(cols, 2 * rows)
+        grad = lax.dot_general(grad, table, (((1,), (1,)), ((), ())), precision=HIGH).astype(BF16)
+        grad = grad.reshape(vis, part, wavs, 2 * m).transpose(2, 0, 1, 3)
+    grad = lax.all_to_all(grad, "wav", split_axis=0, concat_axis=0, tiled=True)
+    if fast:
+        grad = rows_inverse_fast(grad, rows_high_low, twist)
+    else:
+        grad = grad.astype(F32).transpose(1, 0, 2, 3).reshape(vis, rows, 2 * m)
+        grad = rows_inverse(grad, vis).astype(BF16)
     grad = lax.all_to_all(grad, "vis", split_axis=0, concat_axis=0, tiled=True)
     grad = grad.transpose(1, 0, 2).reshape(rows, cols)
     grad = lax.dot_general(grad, spread.astype(BF16), (((1,), (1,)), ((), ())), preferred_element_type=F32)
     shifted = image - grad
-    halo = 8
-    right = lax.ppermute(shifted[:, :halo], "wav", [(i, (i - 1) % wavs) for i in range(wavs)])
-    left = lax.ppermute(shifted[:, -halo:], "wav", [(i, (i + 1) % wavs) for i in range(wavs)])
+    right = lax.ppermute(shifted[:, :HALO], "wav", [(i, (i - 1) % wavs) for i in range(wavs)])
+    left = lax.ppermute(shifted[:, -HALO:], "wav", [(i, (i + 1) % wavs) for i in range(wavs)])
     return haar_mean(shifted, left, right, thresholds), misfit
 
 

time: 550 us -> 362 us (0.66)
  other arithmetic: 142 us -> 48.7 us
  local copies, waits for them, and re-layouts: 95.3 us -> 4.5 us
  matrix products: 79.8 us -> 11.2 us
  Pallas kernels: 0 us -> 57.3 us
  blocking collectives: 62.1 us -> 69 us
  between operations: 14.9 us -> 21.7 us
    dot_general x10 -> x0, matrix products: 68.9 us -> none  [the longest x1 9.98 us: shards(): z = jnp.dot(y, table, precision=HIGH)]
    pallas_call x0 -> x5, Pallas kernels: none -> 57.3 us  [the longest x1 18.1 us: shares_fast(): pl.pallas_call(shares_kernel, in_specs=[pl.BlockSpec(memory_space=pltpu.S...]
    scatter-add x1 -> x0, other arithmetic: 39.8 us -> none  [shards(): jnp.zeros((across * down, vis, low, 2 * PATCH), F32)]
    sub x3 -> x2, other arithmetic: 33.3 us -> 0.01 us  [the longest x1 0.01 us: twist_table(): return cosine(n * (k % groups) - k // groups * (count // 4), count)]
    convert_element_type x0 -> x5, other arithmetic: none -> 31.7 us  [the longest x2 23.9 us: split(): return (high.astype(BF16), (x - high).astype(BF16))]
    slice x11 -> x2, local copies, waits for them, and re-layouts: 29 us -> 0.74 us  [the longest x1 0.6 us: haar_limits(): limit = jnp.where(index == s, thresholds[s] * scale, limit)]
    mul x6 -> x1, other arithmetic: 17 us -> 1.02 us  [cosine(): return value * part]
    reshape x5 -> x0, local copies, waits for them, and re-layouts: 15.2 us -> none  [the longest x1 6.49 us: column_matrix(): return jnp.concatenate([from_re, from_im], 1).reshape(2 * size, 2 * size)]
  transfers between devices with their start and end apart: 7 -> 7, of which waited for: 6 -> 5; matrix products, arithmetic and copies ran while one was open for 5% -> 9% of each run, Pallas kernels for 0% -> 0%
where the time goes in v2:
time: 362 us; the launch traced here: 361 us
  waiting for transfers between devices  126 us (35%)
  blocking collectives  69 us (19%)
  Pallas kernels  57.3 us (16%)
  other arithmetic  48.7 us (13%)
  starting transfers between devices  22.4 us (6%)
  between operations  21.7 us (6%)
  matrix products  11.2 us (3%)
  local copies, waits for them, and re-layouts  4.5 us (1%)
    all_to_all x1, blocking collectives, shards(): grad = lax.all_to_all(grad, 'wav', split_axis=0, concat_axis=0, tiled=True)  53.4 us
    all_to_all x1, waiting for transfers between devices, shards(): lax.all_to_all(tiles.astype(F16), 'vis', split_axis=0, concat_axis=0, til...  46.2 us
    all_gather x1, waiting for transfers between devices, shards(): terms = lax.all_gather(terms, 'vis', axis=0, tiled=True)  35 us
    all_to_all x1, waiting for transfers between devices, shards(): lax.all_to_all(y, 'wav', split_axis=0, concat_axis=0, tiled=True)  28.6 us
    convert_element_type x2, other arithmetic, split(): return (high.astype(BF16), (x - high).astype(BF16))  23.9 us
    pallas_call x1, Pallas kernels, shares_fast(): pl.pallas_call(shares_kernel, in_specs=[pl.BlockSpec(memory_space=pltpu.S...  18.1 us
    all_gather x1, blocking collectives, shards(): ids = lax.all_gather(ids, 'vis', axis=0, tiled=True)  15.7 us
    pallas_call x1, Pallas kernels, gather_fast(): pl.pallas_call(gather_kernel, in_specs=[pl.BlockSpec(memory_space=pltpu.S...  13.9 us
  transfers between devices with their start and end apart: 7, of which 5 were waited for; matrix products, arithmetic and copies ran while one was open for 9% of the time, Pallas kernels for 0%

profile of v2, /device:TPU:2, one launch (start us, length us, event | category | flops | bytes accessed | tf_op | source)
XLA Modules:
  0.0 361.0 jit_solution(9277464626935404642)
XLA Ops:
  7.2 0.0 copy-start
  7.2 4.7 %fusion.55 = f16[1024,512]{1,0:T(8,128)(2,1)S(1)} fusion(f32[512,1024]{1,0:T(8,128)} %param.7, s32[1024]{0:T(1024)S(1)} %fusion.98), kind=kOutput, calls=%fused_computation.116 | convolution fusion | flops 3223846912 | bytes 3149824 | tf_op jit(solution)/shard_map/dot_general | solution.py:407
  11.9 1.6 copy.23
  13.5 4.3 %all-to-all-start = ((f16[8,512,128]{2,1,0:T(8,128)(2,1)}), f16[8,512,128]{2,1,0:T(8,128)(2,1)S(1)}, u32[]{:S(2)}, u32[]{:S(2)}) async-start(f16[8,512,128]{2,1,0:T(8,128)(2,1)} %bitcast.5), calls=%async_computation | async-start | bytes 2097152 | tf_op jit(solution)/shard_map/all_to_all | solution.py:409
  17.9 15.7 %all-gather = s32[8,32,2]{1,2,0:T(2,128)S(1)} all-gather(s32[1,32,2]{1,2,0:T(2,128)S(1)} %add_bitcast_fusion), channel_id=1, replica_groups=mesh['vis'=8,'wav'=4] {'vis'}, dimensions={0}, use_global_device_ids=true | all-gather | bytes 2304 | tf_op jit(solution)/shard_map/all_gather | solution.py:403
  33.6 0.1 reshape.259
  33.7 0.6 and_select_fusion.4
  34.3 0.6 fusion.76
  34.9 0.9 pad_maximum_fusion.2
  35.8 1.0 add_multiply_fusion.3.twist_ref
  36.8 3.9 %fusion.35 = (bf16[1024,512]{1,0:T(8,128)(2,1)}, bf16[1024,512]{1,0:T(8,128)(2,1)}) fusion(s32[1024]{0:T(1024)S(1)} %get-tuple-element.29, s32[1024]{0:T(1024)S(1)} %get-tuple-element.32, pred[1024]{0:T(1024)(128)(4,1)S(1)} %get-tuple-element.33, s32[1024]{0:T(1024)S(1)} %get-tuple-element.30, s32[1024]{0:T(1024)S(1)} %get-tuple-element.31, ...), kind=kLoop, calls=%fused_computation.88 | loop fusion | flops 20971520 | bytes 2115584 | tf_op jit(solution)/shard_map/convert_element_type | solution.py:77
  40.7 1.5 convert_element_type.106.x_ref
  42.2 8.6 %rows_forward.1 = f32[4,8,128,256]{3,2,1,0:T(8,128)} custom-call(f32[8,512,128]{2,1,0:T(8,128)} %convert_element_type.106.x_ref, bf16[1024,512]{1,0:T(8,128)(2,1)} %get-tuple-element.17.high_ref, bf16[1024,512]{1,0:T(8,128)(2,1)} %get-tuple-element.16.low_ref, f32[512,16]{1,0:T(8,128)} %add_multiply_fusion.3.twist_ref), custom_call_target="tpu_custom_call" | custom-call | tf_op jit(solution)/shard_map/rows_forward/pallas_call | solution.py:159
  50.8 3.9 %convert_element_type.111 = f16[4,8,128,256]{3,2,1,0:T(8,128)(2,1)} convert(f32[4,8,128,256]{3,2,1,0:T(8,128)} %rows_forward.1) | non-fusion elementwise | flops 1048576 | bytes 6291456 | tf_op jit(solution)/shard_map/convert_element_type | solution.py:412
  54.7 4.9 %all-to-all-start.1 = ((f16[4,8,128,256]{3,2,1,0:T(8,128)(2,1)}), f16[4,8,128,256]{3,2,1,0:T(8,128)(2,1)S(1)}, u32[]{:S(2)}, u32[]{:S(2)}) async-start(f16[4,8,128,256]{3,2,1,0:T(8,128)(2,1)} %convert_element_type.111), calls=%async_computation.1 | async-start | bytes 4194304 | tf_op jit(solution)/shard_map/all_to_all | solution.py:416
  59.6 20.0 %fusion.1 = (bf16[1024,1024]{1,0:T(8,128)(2,1)}, bf16[1024,1024]{1,0:T(8,128)(2,1)}, bf16[1024,1024]{1,0:T(8,128)(2,1)}, bf16[1024,1024]{1,0:T(8,128)(2,1)}) fusion(s32[1024]{0:T(1024)S(1)} %get-tuple-element.41, s32[1024]{0:T(1024)S(1)} %get-tuple-element.48, pred[1024]{0:T(1024)(128)(4,1)S(1)} %get-tuple-element.51, s32[1024]{0:T(1024)S(1)} %get-tuple-element.44, ...), kind=kLoop, calls=%fused_computation.36 | loop fusion | flops 146800640 | bytes 8434688 | tf_op jit(solution)/shard_map/convert_element_type | solution.py:77
  79.6 28.6 %all-to-all-done.1 = f16[4,8,128,256]{3,2,1,0:T(8,128)(2,1)S(1)} async-done(((f16[4,8,128,256]{3,2,1,0:T(8,128)(2,1)}), f16[4,8,128,256]{3,2,1,0:T(8,128)(2,1)S(1)}, u32[]{:S(2)}, u32[]{:S(2)}) %all-to-all-start.1) | async-done | bytes 2097184 | tf_op jit(solution)/shard_map/all_to_all | solution.py:416
  108.2 2.4 convert_element_type.112.y_ref
  110.6 18.1 %shares.1 = f32[256,64,128]{2,1,0:T(8,128)} custom-call(s32[256]{0:T(256)} %get-tuple-element.24.a_ref, s32[256]{0:T(256)} %get-tuple-element.23.b_ref, f32[4,8,128,256]{3,2,1,0:T(8,128)} %convert_element_type.112.y_ref, bf16[1024,1024]{1,0:T(8,128)(2,1)} %get-tuple-element.13.high_ref, bf16[1024,1024]{1,0:T(8,128)(2,1)} %get-tuple-element.15.low_ref, ...), custom_call_target="tpu_custom_call" | custom-call | tf_op jit(solution)/shard_map/shares/pallas_call | solution.py:206
  128.6 6.5 %convert_element_type.117 = f16[256,64,128]{2,1,0:T(8,128)(2,1)} convert(f32[256,64,128]{2,1,0:T(8,128)} %shares.1) | non-fusion elementwise | flops 2097152 | bytes 12582912 | tf_op jit(solution)/shard_map/convert_element_type | solution.py:429
  135.2 7.2 %all-to-all-start.2 = ((f16[256,64,128]{2,1,0:T(8,128)(2,1)}), f16[256,64,128]{2,1,0:T(8,128)(2,1)}, u32[]{:S(2)}, u32[]{:S(2)}) async-start(f16[256,64,128]{2,1,0:T(8,128)(2,1)} %convert_element_type.117), calls=%async_computation.2 | async-start | bytes 8388608 | tf_op jit(solution)/shard_map/all_to_all | solution.py:429
  142.3 1.5 bitcast_convert_fusion
  143.8 46.2 %all-to-all-done.2 = f16[256,64,128]{2,1,0:T(8,128)(2,1)} async-done(((f16[256,64,128]{2,1,0:T(8,128)(2,1)}), f16[256,64,128]{2,1,0:T(8,128)(2,1)}, u32[]{:S(2)}, u32[]{:S(2)}) %all-to-all-start.2) | async-done | bytes 4194336 | tf_op jit(solution)/shard_map/all_to_all | solution.py:429
  190.0 3.2 convert_reduce_fusion
  193.3 0.8 fusion.44
  194.1 1.0 fusion.45
  195.1 0.8 convolution_convert_fusion.1
  195.9 0.8 convolution_convert_fusion
  196.6 1.1 pad_maximum_fusion
  197.7 0.0 all-gather.3.cloned.1.call-update
  197.8 35.0 %all-gather.3.cloned.1.call-done.term_ref = bf16[256,64,128]{2,1,0:T(8,128)(2,1)} async-done(((bf16[32,64,128]{2,1,0:T(8,128)(2,1)}), bf16[256,64,128]{2,1,0:T(8,128)(2,1)}) %all-gather.3.cloned.1.call-update) | async-done | bytes 4194320 | tf_op jit(solution)/shard_map/all_gather | solution.py:443
  232.7 13.9 %gather.1 = bf16[4,8,128,256]{3,2,1,0:T(8,128)(2,1)} custom-call(s32[256]{0:T(256)} %get-tuple-element.24.a_ref, s32[256]{0:T(256)} %get-tuple-element.23.b_ref, bf16[256,64,128]{2,1,0:T(8,128)(2,1)} %all-gather.3.cloned.1.call-done.term_ref, bf16[1024,1024]{1,0:T(8,128)(2,1)} %get-tuple-element.14.high_ref, bf16[1024,1024]{1,0:T(8,128)(2,1)} %get-tuple-element.12.low_ref, ...), custom_call_target="tpu_custom_call" | custom-call | tf_op jit(solution)/shard_map/gather/pallas_call | solution.py:248
  246.7 53.4 %all_to_all.25.y_ref = bf16[4,8,128,256]{3,2,1,0:T(8,128)(2,1)} all-to-all(bf16[4,8,128,256]{3,2,1,0:T(8,128)(2,1)} %gather.1), channel_id=1, replica_groups=mesh['vis'=8,'wav'=4] {'wav'}, dimensions={0} | all-to-all | bytes 4194304 | tf_op jit(solution)/shard_map/all_to_all | solution.py:454
  300.0 8.0 %rows_inverse.1 = bf16[8,512,128]{2,1,0:T(8,128)(2,1)} custom-call(bf16[4,8,128,256]{3,2,1,0:T(8,128)(2,1)} %all_to_all.25.y_ref, bf16[1024,512]{1,0:T(8,128)(2,1)} %get-tuple-element.17.high_ref, bf16[1024,512]{1,0:T(8,128)(2,1)} %get-tuple-element.16.low_ref, f32[512,16]{1,0:T(8,128)} %add_multiply_fusion.3.twist_ref), custom_call_target="tpu_custom_call" | custom-call | tf_op jit(solution)/shard_map/rows_inverse/pallas_call | solution.py:289
  308.0 4.0 %all-to-all-start.4 = ((bf16[8,512,128]{2,1,0:T(8,128)(2,1)}), bf16[8,512,128]{2,1,0:T(8,128)(2,1)S(1)}, u32[]{:S(2)}, u32[]{:S(2)}) async-start(bf16[8,512,128]{2,1,0:T(8,128)(2,1)} %rows_inverse.1), calls=%async_computation.4 | async-start | bytes 2097152 | tf_op jit(solution)/shard_map/all_to_all | solution.py:460
  312.1 0.6 fusion.104
  320.2 5.8 %all-to-all-done.4 = bf16[8,512,128]{2,1,0:T(8,128)(2,1)S(1)} async-done(((bf16[8,512,128]{2,1,0:T(8,128)(2,1)}), bf16[8,512,128]{2,1,0:T(8,128)(2,1)S(1)}, u32[]{:S(2)}, u32[]{:S(2)}) %all-to-all-start.4) | async-done | bytes 1048608 | tf_op jit(solution)/shard_map/all_to_all | solution.py:460
  326.0 1.3 copy.27
  327.3 3.2 fusion.54.refs_0_
  330.5 0.1 fusion.103
  330.6 1.5 collective-permute-start
  332.1 0.6 collective-permute-start.1
  332.7 0.6 pad_maximum_fusion.4.refs_2_
  333.3 0.1 pad.5.clone
  333.4 0.7 copy.28
  334.1 10.5 %collective-permute-done = f32[512,8]{1,0:T(8,128)S(1)} collective-permute-done((f32[512,8]{1,0:T(8,128)S(1)}, f32[512,8]{1,0:T(8,128)S(1)}, u32[]{:S(2)}, u32[]{:S(2)}) %collective-permute-start) | collective-permute-done | bytes 16416 | tf_op jit(solution)/shard_map/ppermute | solution.py:464
  344.6 0.8 pad_maximum_fusion.1.refs_1_
  345.4 8.7 %haar.1 = f32[512,1024]{1,0:T(8,128)} custom-call(f32[512,1024]{1,0:T(8,128)} %copy-done.1, f32[512,128]{1,0:T(8,128)} %pad_maximum_fusion.1.refs_1_, f32[4,1152]{1,0:T(4,128)} %pad_maximum_fusion.4.refs_2_), custom_call_target="tpu_custom_call" | custom-call | tf_op jit(solution)/shard_map/haar/pallas_call | solution.py:373
  (37 shorter events, 0.2 us)
Async XLA Ops:
  7.2 186.1 %copy-start = (bf16[32,64,256]{2,1,0:T(8,128)(2,1)S(1)}, bf16[32,64,256]{2,1,0:T(8,128)(2,1)}, u32[]{:S(2)}) copy-start(bf16[32,64,256]{2,1,0:T(8,128)(2,1)} %param.8) | copy-start | bytes 3145732
  7.2 10.7 %copy-start.4 = (s32[32]{0:T(128)S(1)}, s32[32]{0:T(128)}, u32[]{:S(2)}) copy-start(s32[32]{0:T(128)} %param.12) | copy-start | bytes 388
  7.2 10.7 %copy-start.5 = (s32[32,1]{0,1:T(1,128)S(1)}, s32[32,1]{0,1:T(1,128)}, u32[]{:S(2)}) copy-start(s32[32,1]{0,1:T(1,128)} %param.11) | copy-start | bytes 388
  13.5 27.2 %all-to-all-start = ((f16[8,512,128]{2,1,0:T(8,128)(2,1)}), f16[8,512,128]{2,1,0:T(8,128)(2,1)S(1)}, u32[]{:S(2)}, u32[]{:S(2)}) async-start(f16[8,512,128]{2,1,0:T(8,128)(2,1)} %bitcast.5), calls=%async_computation | async-start | bytes 2097152 | tf_op jit(solution)/shard_map/all_to_all | solution.py:409
  54.7 53.5 %all-to-all-start.1 = ((f16[4,8,128,256]{3,2,1,0:T(8,128)(2,1)}), f16[4,8,128,256]{3,2,1,0:T(8,128)(2,1)S(1)}, u32[]{:S(2)}, u32[]{:S(2)}) async-start(f16[4,8,128,256]{3,2,1,0:T(8,128)(2,1)} %convert_element_type.111), calls=%async_computation.1 | async-start | bytes 4194304 | tf_op jit(solution)/shard_map/all_to_all | solution.py:416
  135.2 54.9 %all-to-all-start.2 = ((f16[256,64,128]{2,1,0:T(8,128)(2,1)}), f16[256,64,128]{2,1,0:T(8,128)(2,1)}, u32[]{:S(2)}, u32[]{:S(2)}) async-start(f16[256,64,128]{2,1,0:T(8,128)(2,1)} %convert_element_type.117), calls=%async_computation.2 | async-start | bytes 8388608 | tf_op jit(solution)/shard_map/all_to_all | solution.py:429
  142.3 90.4 %all-gather.3.cloned.1.call-start = ((), (), s32[]{:S(2)}) async-start(), calls=%async_computation.5 | async-start | bytes 4718592 | tf_op jit(solution)/shard_map/all_gather | solution.py:443
  193.3 1.8 copy-start.2
  300.0 12.0 %copy-start.3 = (f32[4]{0:T(128)S(1)}, f32[4]{0:T(128)}, u32[]{:S(2)}) copy-start(f32[4]{0:T(128)} %param.13) | copy-start | bytes 52
  308.0 17.9 %all-to-all-start.4 = ((bf16[8,512,128]{2,1,0:T(8,128)(2,1)}), bf16[8,512,128]{2,1,0:T(8,128)(2,1)S(1)}, u32[]{:S(2)}, u32[]{:S(2)}) async-start(bf16[8,512,128]{2,1,0:T(8,128)(2,1)} %rows_inverse.1), calls=%async_computation.4 | async-start | bytes 2097152 | tf_op jit(solution)/shard_map/all_to_all | solution.py:460
  330.5 15.0 %copy-start.1 = (f32[512,1024]{1,0:T(8,128)}, f32[512,1024]{1,0:T(8,128)S(1)}, u32[]{:S(2)}) copy-start(f32[512,1024]{1,0:T(8,128)S(1)} %fusion.54.refs_0_) | copy-start | bytes 6291460
  330.6 13.9 %collective-permute-start = (f32[512,8]{1,0:T(8,128)S(1)}, f32[512,8]{1,0:T(8,128)S(1)}, u32[]{:S(2)}, u32[]{:S(2)}) collective-permute-start(f32[512,8]{1,0:T(8,128)S(1)} %get-tuple-element.8), channel_id=1, source_target_pairs={{0,3},{1,0},{2,1},{3,2},{4,7},{5,4},{6,5},{7,6},{8,11},{9,8},{10,9... | collective-permute-start | bytes 49160 | tf_op jit(solution)/shard_map/ppermute | solution.py:464
  332.1 12.5 %collective-permute-start.1 = (f32[512,8]{1,0:T(8,128)S(1)}, f32[512,8]{1,0:T(8,128)S(1)}, u32[]{:S(2)}, u32[]{:S(2)}) collective-permute-start(f32[512,8]{1,0:T(8,128)S(1)} %get-tuple-element.9), channel_id=1, source_target_pairs={{0,1},{1,2},{2,3},{3,0},{4,5},{5,6},{6,7},{7,4},{8,9},{9,10},{10,1... | collective-permute-start | bytes 49160 | tf_op jit(solution)/shard_map/ppermute | solution.py:465
Sparse Core Ops, SparseCore 0:
  197.9 34.7 all-gather.2
